TPU v7x, 32 devices: a whole 2x2x4 slice. The times are simulated.
32 devices in a mesh: lvl: 2 (over x), lat: 4 (over z), lon: 4 (over y, core).
Axes of the slice: x: 2, y: 2, z: 4, core: 2. Of those that a mesh axis runs over, the one named last changes fastest.
Arguments:
- patches: bfloat16 [2, 2, 24, 48, 1000], P('lvl', None, 'lat', 'lon'), may hold values from -6 to 6
- level_embed: float32 [2, 512], P('lvl'), may hold values from -6 to 6
- embed_weight: bfloat16 [1000, 512], replicated, may hold values from -0.1875 to 0.1875
- block_ids: int32 [2, 2, 4, 4, 3], P('lvl', None, 'lat', 'lon'), may hold values from -1 to 5, as said below
- latent_queries: bfloat16 [4, 512], replicated, may hold values from -6 to 6
- cross_gain: float32 [512], replicated, may hold values from 0.1 to 1.9
- cross_query: bfloat16 [512, 512], replicated, may hold values from -0.25 to 0.25
- cross_kv: bfloat16 [512, 1024], replicated, may hold values from -0.25 to 0.25
- cross_out: bfloat16 [512, 512], replicated, may hold values from -0.25 to 0.25
- region_ids: int32 [48, 48], P(('lvl', 'lat'), 'lon'), may hold values from 0 to 2
- swin_gain: float32 [512], replicated, may hold values from 0.1 to 1.9
- swin_qkv: bfloat16 [512, 1536], replicated, may hold values from -0.25 to 0.25
- swin_out: bfloat16 [512, 512], replicated, may hold values from -0.25 to 0.25
- mlp_gain: float32 [512], replicated, may hold values from 0.1 to 1.9
- mlp_up: bfloat16 [512, 2048], replicated, may hold values from -0.25 to 0.25
- mlp_down: bfloat16 [2048, 512], replicated, may hold values from -0.125 to 0.125
Outputs:
- latents: float32 [4, 48, 48, 512], P(None, ('lvl', 'lat'), 'lon')
Inputs may be any that keep to these rules, and one draw needn't show every extreme that they name: block_ids[l, m, a, o, :] lists the column blocks b (longitude column (m * 4 + a) * 6 + b, latitude rows o * 12 to o * 12 + 11) at which level l is present: distinct numbers in its first slots, -1 in the remaining slots. Every column block is named by the list of at least one level. For every band and tile, the list of some level fills all 3 slots.
All inputs are finite; a program needn't handle non-finite values.
Results may differ from a plain program's by a relative error of at most 0.005.
Values may be sent and summed in bfloat16 or wider, within the bound.
A program may use at most 64 MiB of HBM per device.

v0:
```python
import functools
import math

import jax
import jax.numpy as jnp
import numpy as np
from jax import lax
from jax.experimental import pallas as pl
from jax.experimental.pallas import tpu as pltpu
from jax.sharding import PartitionSpec as P

HEADS = 16
WIN_LAT = 6
BLOCK = 16
CODE = 64
MESH = pl.DeviceIdType.MESH
F32 = jnp.float32
BF16 = jnp.bfloat16


def layer_norm(tensor, gain_vec):
    average = jnp.mean(tensor, axis=-1, keepdims=True)
    centred = tensor - average
    spread = jnp.mean(centred * centred, axis=-1, keepdims=True)
    return centred * lax.rsqrt(spread + 1e-05) * gain_vec


def mm(a, b):
    return jnp.dot(a, b, preferred_element_type=F32)


def mm_nt(a, b):
    return lax.dot_general(a, b, (((1,), (1,)), ((), ())), preferred_element_type=F32)


class Plan:
    def __init__(self, rows, cols, cap):
        self.rows, self.cols, self.cap = rows, cols, cap
        self.margin = WIN_LAT // 2
        per = (BLOCK - 1) // cap
        assert per >= self.margin and rows < CODE and rows * cols <= 128
        self.blocks = max(2, -(-cols // per))
        spread = [min(per, cols)]
        middle = cols - 2 * per
        assert middle >= 0
        groups = [list(range(per))]
        groups += [list(range(c, min(c + per, cols - per))) for c in range(per, cols - per, per)]
        groups += [list(range(cols - per, cols))]
        self.blocks = len(groups)
        self.tile_rows = self.blocks * BLOCK
        col_of = np.full((self.blocks, BLOCK), -1)
        for b, group in enumerate(groups):
            for k, c in enumerate(group):
                col_of[b, k * cap : (k + 1) * cap] = c
        self.col_of = col_of.reshape(-1)
        self.tiles = [(0, self.tile_rows), (self.tile_rows, self.tile_rows)]
        self.tiles += [(2 * self.tile_rows + k * BLOCK, BLOCK) for k in range(4)]
        self.wide_rows = 2 * self.tile_rows + 4 * BLOCK
        first, last = self.col_of[:BLOCK], self.col_of[-BLOCK:]
        parts = [self.col_of, self.col_of, last, last, first, first]
        row_code = np.concatenate(
            [np.where(p >= 0, (t * cols + p) * CODE, -100000) for t, p in enumerate(parts)]
        )
        lanes = -(-self.wide_rows // 128) * 128
        self.lanes = lanes
        self.row_code = np.full((8, lanes), -100000, np.int32)
        self.row_code[:, : self.wide_rows] = row_code
        m = self.margin
        spans = [range(cols), range(cols), range(cols - m, cols), range(cols - m, cols), range(m), range(m)]
        offset = [0, 0, -cols, -cols, cols, cols]
        cells = [(t, i, j, (j + offset[t] + m) // WIN_LAT) for t in range(6) for i in range(rows) for j in spans[t]]
        self.cells = np.array(cells)
        self.count = len(cells)
        self.own = rows * cols
        self.info = np.zeros((self.count, 128), np.int32)
        t, i, j, win = self.cells.T
        self.info[:, 0] = (t * cols + j) * CODE + i
        self.info[:, 1] = i * cols + j
        self.info[:, 2] = t
        self.win = (win[: self.own, None] == win[None, :]).astype(np.float32)


def send_kernel(plan, names, sizes, patches, level_embed, weight, ids, labels, out, wbuf, buf, wsem, send, recv, local):
    rows, cols, cap = plan.rows, plan.cols, plan.cap
    levels, lat_count, lon_count = sizes
    width = weight.shape[1]
    load = pltpu.make_async_copy(weight, wbuf, wsem)
    load.start()
    me_l, me_a, me_o = (lax.axis_index(name) for name in names)
    low_bit = lax.rem(me_a, 2)
    partner = me_a + 1 - 2 * low_bit
    lats = (me_a, partner)
    lons = {
        0: me_o,
        1: lax.rem(me_o + 1, lon_count),
        -1: lax.rem(me_o + lon_count - 1, lon_count),
    }
    moves = [
        (dm, da, do)
        for dm in range(levels)
        for da in (0, 1)
        for do in (0, -1, 1)
        if (dm, da, do) != (0, 0, 0)
    ]
    band_of = [lax.rem(me_l + dm, levels) for dm in range(levels)]
    barrier = pltpu.get_barrier_semaphore()
    for dm, da, do in moves:
        pl.semaphore_signal(
            barrier, inc=1, device_id=(band_of[dm], lats[da], lons[do]), device_id_type=MESH
        )

    tile_rows = plan.tile_rows
    row = lax.broadcasted_iota(jnp.int32, (tile_rows, 1), 0)
    col_of = jnp.full((tile_rows, 1), -1, jnp.int32)
    slot_of = jnp.full((tile_rows, 1), -1, jnp.int32)
    for r in range(tile_rows):
        pass
    in_block = jnp.bitwise_and(row, BLOCK - 1)
    base = jnp.zeros((tile_rows, 1), jnp.int32)
    for b in range(plan.blocks):
        start = int(plan.col_of[b * BLOCK])
        base = jnp.where((row >= b * BLOCK) & (row < (b + 1) * BLOCK), start, base)
    col_step = jnp.zeros((tile_rows, 1), jnp.int32)
    for k in range(1, BLOCK // cap + 1):
        col_step = col_step + (in_block >= k * cap).astype(jnp.int32)
    slot_of = in_block - col_step * cap
    col_of = base + col_step
    used = jnp.zeros((tile_rows, 1), jnp.bool_)
    for b in range(plan.blocks):
        n = int((plan.col_of[b * BLOCK : (b + 1) * BLOCK] >= 0).sum())
        used = used | ((row >= b * BLOCK) & (row < b * BLOCK + n))
    cell = lax.broadcasted_iota(jnp.int32, (128, 1), 0)
    cell_i = jnp.zeros((128, 1), jnp.int32)
    for k in range(1, rows):
        cell_i = cell_i + (cell >= k * cols).astype(jnp.int32)
    cell_j = cell - cell_i * cols
    lab = labels[...].astype(F32)
    col_lab = jnp.zeros((128, cols), F32)
    for k in range(rows):
        col_lab = jnp.where(cell_i == k, lab[k : k + 1, :], col_lab)
    picked_j = lax.broadcasted_iota(jnp.int32, (128, cols), 1) == cell_j
    lab_col = jnp.sum(jnp.where(picked_j, col_lab, 0.0), axis=1, keepdims=True)
    eye = lax.broadcasted_iota(jnp.int32, (128, 128), 0) == lax.broadcasted_iota(jnp.int32, (128, 128), 1)
    lab_row = jnp.sum(jnp.where(eye, lab_col, 0.0), axis=0, keepdims=True)
    lane = lax.broadcasted_iota(jnp.int32, (1, plan.lanes), 1)
    lane_in = jnp.bitwise_and(lane, BLOCK - 1)
    lane_step = jnp.zeros_like(lane)
    for k in range(1, BLOCK // cap + 1):
        lane_step = lane_step + (lane_in >= k * cap).astype(jnp.int32)
    lane_slot = lane_in - lane_step * cap

    id_cols, metas = [], []
    for band in range(levels):
        id_col = jnp.full((tile_rows, 1), -1, jnp.int32)
        id_row = jnp.full((1, plan.lanes), -1, jnp.int32)
        for s in range(cap):
            number = ids[0, band, 0, 0, s]
            id_col = jnp.where(slot_of == s, number, id_col)
            id_row = jnp.where(lane_slot == s, number, id_row)
        id_cols.append(jnp.where(used, id_col, -1))
        pad = jnp.zeros((1, width - plan.lanes - 128), F32)
        metas.append(jnp.concatenate([id_row.astype(F32), lab_row, pad], axis=1))
    wanted = jnp.concatenate([col_of * levels + band for band in range(levels)], axis=0)
    source = lax.broadcasted_iota(jnp.int32, (levels * tile_rows, cols * levels), 1)
    same_col = source == wanted
    id_all = jnp.concatenate(id_cols, axis=0)
    stacked = jnp.zeros((levels * tile_rows, patches.shape[-1]), F32)
    for i in range(rows):
        chosen = jnp.where(same_col & (id_all == i), 1.0, 0.0).astype(BF16)
        stacked = stacked + mm(chosen, patches[i].reshape(cols * levels, patches.shape[-1]))
    stacked = stacked.astype(BF16)
    load.wait()
    embedded = mm(stacked, wbuf[...]) + level_embed[...]
    for band in range(levels):
        part = embedded[band * tile_rows : (band + 1) * tile_rows]
        buf[band] = jnp.where(in_block == BLOCK - 1, metas[band], part).astype(BF16)
    pl.semaphore_wait(barrier, len(moves))
    copies = []
    for k, (dm, da, do) in enumerate(moves):
        if do == 0:
            source, target, count = 0, plan.tiles[da][0], tile_rows
        elif do == 1:
            source, target, count = tile_rows - BLOCK, plan.tiles[2 + da][0], BLOCK
        else:
            source, target, count = 0, plan.tiles[4 + da][0], BLOCK
        copies.append(
            pltpu.make_async_remote_copy(
                src_ref=buf.at[band_of[dm], pl.ds(source, count)],
                dst_ref=out.at[me_l, pl.ds(target, count)],
                send_sem=send.at[k],
                recv_sem=recv.at[k],
                device_id=(band_of[dm], lats[da], lons[do]),
                device_id_type=MESH,
            )
        )
    for copy in copies[::-1]:
        copy.start()
    own = pltpu.make_async_copy(buf.at[me_l], out.at[me_l, pl.ds(0, tile_rows)], local)
    own.start()
    own.wait()
    for copy in copies:
        copy.wait()


def main_kernel(
    plan, names, sizes, wide, info, row_code, win, hm, lq, cross_gain, swin_gain, mlp_gain,
    cross_kv, cross_query, cross_out, swin_qkv, swin_out, mlp_up, mlp_down,
    out,
    b_kv, b_query, b_out, b_qkv, b_so, b_up, b_down, start, sems,
):
    levels, _, lon_count = sizes
    pairs = [
        (cross_query, b_query), (cross_kv, b_kv), (cross_out, b_out), (swin_qkv, b_qkv),
        (swin_out, b_so), (mlp_up, b_up), (mlp_down, b_down),
    ]
    loads = [pltpu.make_async_copy(a, b, sems.at[k]) for k, (a, b) in enumerate(pairs)]
    for load in loads:
        load.start()
    l_query, l_kv, l_out, l_qkv, l_so, l_up, l_down = loads
    me_l, me_o = lax.axis_index(names[0]), lax.axis_index(names[2])
    width = lq.shape[1]
    head_dim = width // HEADS
    inv_root = 1.0 / math.sqrt(head_dim)
    latents = lq.shape[0]
    own, count = plan.own, plan.count
    lanes = plan.lanes
    code_c = info[:, 0:1]
    pos_c = info[:, 1:2]
    tile_c = info[:, 2:3]
    lane = lax.broadcasted_iota(jnp.int32, (1, lanes), 1)
    meta_rows = [first + BLOCK - 1 for first, _ in plan.tiles]

    lq_f = lq[...].astype(F32)
    l_query.wait()
    cq = (mm(lq[...], b_query[...]) * inv_root).astype(BF16).astype(F32)
    hm_f = hm[...].astype(F32)
    masked = jnp.concatenate([cq[q : q + 1] * hm_f for q in range(latents)], axis=0).astype(BF16)

    l_kv.wait()
    keys, values, presence = [], [], []
    for level in range(levels):
        tokens = wide[level].astype(F32)
        keys_in = layer_norm(tokens, cross_gain[...]).astype(BF16)
        pair = mm(keys_in, b_kv[...]).astype(BF16)
        id_row = tokens[meta_rows[0] : meta_rows[0] + 1, :lanes]
        for t in range(1, 6):
            first, _ = plan.tiles[t]
            id_row = jnp.where(lane >= first, tokens[meta_rows[t] : meta_rows[t] + 1, :lanes], id_row)
        code_r = (row_code[0:1, :] + id_row.astype(jnp.int32))[:, : plan.wide_rows]
        scatter = jnp.where(
            (code_c == code_r) & (id_row.astype(jnp.int32)[:, : plan.wide_rows] >= 0), 1.0, 0.0
        )
        presence.append(jnp.sum(scatter, axis=1, keepdims=True))
        spread = mm(scatter.astype(BF16), pair)
        keys.append(spread[:, :width].astype(BF16))
        values.append(spread[:, width:])
    lab_src = wide[me_l].astype(F32)
    seg = jnp.zeros((count, 128), F32)
    for t in range(6):
        seg = jnp.where(tile_c == t, lab_src[meta_rows[t] : meta_rows[t] + 1, lanes : lanes + 128], seg)
    at_pos = lax.broadcasted_iota(jnp.int32, (count, 128), 1) == pos_c
    lab_col = jnp.sum(jnp.where(at_pos, seg, 0.0), axis=1, keepdims=True)
    eye = lax.broadcasted_iota(jnp.int32, (count, count), 0) == lax.broadcasted_iota(
        jnp.int32, (count, count), 1
    )
    lab_row = jnp.sum(jnp.where(eye, lab_col, 0.0), axis=0, keepdims=True)
    cell_lane = lax.broadcasted_iota(jnp.int32, (1, count), 1)
    halo = (count - 2 * own) // 2
    bad = ((cell_lane >= 2 * own) & (cell_lane < 2 * own + halo) & (me_o == 0)) | (
        (cell_lane >= 2 * own + halo) & (me_o == lon_count - 1)
    )
    lab_row = jnp.where(bad, -1.0, lab_row)
    allowed = jnp.where(lab_col[:own] == lab_row, win[...], 0.0)
    group = 128 // head_dim
    allowed = jnp.concatenate([allowed] * group, axis=0) > 0.5

    exps = [jnp.exp(mm_nt(keys[l], masked)) * presence[l] for l in range(levels)]
    norm = exps[0]
    for e in exps[1:]:
        norm = norm + e
    weights = [(e / norm).astype(BF16) for e in exps]
    hm_all = jnp.concatenate([hm_f] * latents, axis=0)
    hm_row = lax.broadcasted_iota(jnp.int32, hm_all.shape, 0)
    l_out.wait()
    l_qkv.wait()
    queries, wkeys, wvalues = [], [], []
    for q in range(latents):
        expand = jnp.where(
            (hm_row >= q * HEADS) & (hm_row < (q + 1) * HEADS), hm_all, 0.0
        ).astype(BF16)
        mix = mm(weights[0], expand) * values[0]
        for l in range(1, levels):
            mix = mix + mm(weights[l], expand) * values[l]
        latent = mm(mix.astype(BF16), b_out[...]) + lq_f[q : q + 1]
        start[q * own : (q + 1) * own] = latent[:own]
        normed_f = layer_norm(latent, swin_gain[...])
        normed = normed_f.astype(BF16)
        kv = mm(normed, b_qkv[:, width:]).astype(BF16)
        wkeys.append(kv[:, :width])
        wvalues.append(kv[:, width:])
        queries.append(normed_f[:own])
    q_all = mm(jnp.concatenate(queries, axis=0).astype(BF16), b_qkv[:, :width]) * inv_root
    lane_head = [
        (lax.broadcasted_iota(jnp.int32, (1, 128), 1) >= h * head_dim)
        & (lax.broadcasted_iota(jnp.int32, (1, 128), 1) < (h + 1) * head_dim)
        for h in range(group)
    ]
    mixes = []
    for p in range(latents):
        partners = [k for k in range(latents) if (k + 1) // 2 == (p + 1) // 2]
        pieces = []
        for g in range(width // 128):
            cut = slice(g * 128, (g + 1) * 128)
            part = q_all[p * own : (p + 1) * own, cut]
            stack = jnp.concatenate([jnp.where(h, part, 0.0) for h in lane_head], axis=0).astype(BF16)
            raised = [
                jnp.where(allowed, jnp.exp(mm_nt(stack, wkeys[k][:, cut])), 0.0) for k in partners
            ]
            norm = jnp.sum(raised[0], axis=1, keepdims=True)
            for e in raised[1:]:
                norm = norm + jnp.sum(e, axis=1, keepdims=True)
            inverse = 1.0 / norm
            total = mm((raised[0] * inverse).astype(BF16), wvalues[partners[0]][:, cut])
            for e, k in zip(raised[1:], partners[1:]):
                total = total + mm((e * inverse).astype(BF16), wvalues[k][:, cut])
            piece = jnp.zeros((own, 128), F32)
            for h in range(group):
                piece = jnp.where(lane_head[h], total[h * own : (h + 1) * own], piece)
            pieces.append(piece)
        mixes.append(jnp.concatenate(pieces, axis=1))
    l_so.wait()
    attended = start[...] + mm(jnp.concatenate(mixes, axis=0).astype(BF16), b_so[...])
    mlp_in = layer_norm(attended, mlp_gain[...]).astype(BF16)
    l_up.wait()
    l_down.wait()
    hidden = mlp_up.shape[1]
    result = attended
    step = 512
    for c in range(0, hidden, step):
        up = mm(mlp_in, b_up[:, c : c + step])
        act = (up * (1.0 + lax.erf(up * math.sqrt(0.5))) * 0.5).astype(BF16)
        result = result + mm(act, b_down[c : c + step, :])
    for p in range(latents):
        out[:, p, :] = result[p * own : (p + 1) * own]


def shards(
    sizes, names,
    patches, level_embed, embed_weight, block_ids, latent_queries, cross_gain, cross_query, cross_kv,
    cross_out, region_ids, swin_gain, swin_qkv, swin_out, mlp_gain, mlp_up, mlp_down,
):
    levels = sizes[0]
    _, bands, rows, cols, _ = patches.shape
    width = embed_weight.shape[1]
    plan = Plan(rows, cols, block_ids.shape[-1])
    vmem = pl.BlockSpec(memory_space=pltpu.VMEM)
    hbm = pl.BlockSpec(memory_space=pl.ANY)
    moves = 6 * levels - 1
    wide = pl.pallas_call(
        functools.partial(send_kernel, plan, names, sizes),
        out_shape=jax.ShapeDtypeStruct((levels, plan.wide_rows, width), BF16),
        in_specs=[vmem, vmem, hbm, pl.BlockSpec(memory_space=pltpu.SMEM), vmem],
        out_specs=vmem,
        scratch_shapes=[
            pltpu.VMEM(embed_weight.shape, BF16),
            pltpu.VMEM((bands, plan.tile_rows, width), BF16),
            pltpu.SemaphoreType.DMA,
            pltpu.SemaphoreType.DMA((moves,)),
            pltpu.SemaphoreType.DMA((moves,)),
            pltpu.SemaphoreType.DMA,
        ],
        compiler_params=pltpu.CompilerParams(collective_id=0, has_side_effects=True),
        name="send",
    )(patches[0].transpose(1, 2, 0, 3), level_embed, embed_weight, block_ids, region_ids)
    latents = latent_queries.shape[0]
    head_mask = (np.arange(width)[None, :] // (width // HEADS) == np.arange(HEADS)[:, None])
    weights = (cross_kv, cross_query, cross_out, swin_qkv, swin_out, mlp_up, mlp_down)
    tokens = pl.pallas_call(
        functools.partial(main_kernel, plan, names, sizes),
        out_shape=jax.ShapeDtypeStruct((plan.own, latents, width), F32),
        in_specs=[vmem] * 9 + [hbm] * 7,
        out_specs=vmem,
        scratch_shapes=[pltpu.VMEM(w.shape, BF16) for w in weights]
        + [pltpu.VMEM((latents * plan.own, width), F32), pltpu.SemaphoreType.DMA((7,))],
        compiler_params=pltpu.CompilerParams(vmem_limit_bytes=56 << 20),
        name="main",
    )(
        wide, jnp.asarray(plan.info), jnp.asarray(plan.row_code), jnp.asarray(plan.win),
        jnp.asarray(head_mask, BF16), latent_queries, cross_gain.reshape(1, -1),
        swin_gain.reshape(1, -1), mlp_gain.reshape(1, -1), *weights,
    )
    return tokens.reshape(rows, cols, latents, width).transpose(2, 0, 1, 3)


def solution(mesh):
    names = ("lvl", "lat", "lon")
    sizes = tuple(mesh.shape[name] for name in names)
    tiled = P("lvl", None, "lat", "lon", None)
    return jax.shard_map(
        functools.partial(shards, sizes, names),
        mesh=mesh,
        in_specs=(
            tiled, P("lvl", None), P(), tiled, P(), P(), P(), P(), P(), P(("lvl", "lat"), "lon"),
            P(), P(), P(), P(), P(), P(),
        ),
        out_specs=P(None, ("lvl", "lat"), "lon", None),
        check_vma=False,
    )
```

profile of v0, /device:TPU:0, one launch (start us, length us, event | category | flops | bytes accessed | tf_op | source)
XLA Modules:
  0.0 25.4 jit_solution(6319996443917417526)
XLA Ops:
  0.0 12.0 %send.1.wide = bf16[2,160,512]{2,1,0:T(8,128)(2,1)} custom-call(bf16[6,12,2,1000]{3,2,1,0:T(2,128)(2,1)} %bitcast.9, f32[1,512]{1,0:T(1,128)} %level_embed.1, bf16[1000,512]{1,0:T(8,128)(2,1)} %weight.1, s32[1,2,1,1,3]{4,3,2,1,0:T(1,128)} %ids.1, s32[6,12]{1,0:T(8,128)} %labels.1), custom_call_target="tpu_custom_call" | custom-call | tf_op jit(solution)/shard_map/send/pallas_call | solution.py:359
  12.0 13.4 %main.1 = f32[72,4,512]{2,1,0:T(4,128)} custom-call(bf16[2,160,512]{2,1,0:T(8,128)(2,1)} %send.1.wide, s32[216,128]{1,0:T(8,128)} %constant.8.clone.info, s32[8,256]{1,0:T(8,128)} %constant.9.clone.row_code, f32[72,216]{1,0:T(8,128)} %constant.10.clone.win, bf16[16,512]{1,0:T(8,128)(2,1)} %constant.11.clone.hm, bf16[4,512]{1,0:T(4,128)(2,1)} %lq.1, ...), custom_call_target="tpu_custom_call" | custom-call | tf_op jit(solution)/shard_map/main/pallas_call | solution.py:378
where the time goes:
time: 25.6 us; the launch traced here: 25.4 us
  Pallas kernels  25.4 us (99%)
    pallas_call x1, Pallas kernels, shards(): pl.pallas_call(functools.partial(main_kernel, plan, names, sizes), out_sh...  13.4 us
    pallas_call x1, Pallas kernels, shards(): pl.pallas_call(functools.partial(send_kernel, plan, names, sizes), out_sh...  12 us

commit v1 on v0

--- a/solution.py
+++ b/solution.py
@@ -13,6 +13,7 @@
 WIN_LAT = 6
 BLOCK = 16
 CODE = 64
+VMEM = 63700000
 MESH = pl.DeviceIdType.MESH
 F32 = jnp.float32
 BF16 = jnp.bfloat16
@@ -80,12 +81,17 @@
         self.win = (win[: self.own, None] == win[None, :]).astype(np.float32)
 
 
-def send_kernel(plan, names, sizes, patches, level_embed, weight, ids, labels, out, wbuf, buf, wsem, send, recv, local):
+def send_kernel(plan, names, sizes, patches, level_embed, weight, ids, labels, *rest):
+    big = rest[:7]
+    out = rest[7]
+    fast = rest[8:15]
+    wbuf, buf, wsem, send, recv, local, fsem = rest[15:]
     rows, cols, cap = plan.rows, plan.cols, plan.cap
     levels, lat_count, lon_count = sizes
     width = weight.shape[1]
     load = pltpu.make_async_copy(weight, wbuf, wsem)
     load.start()
+    fetch = [pltpu.make_async_copy(a, b, fsem.at[k]) for k, (a, b) in enumerate(zip(big, fast))]
     me_l, me_a, me_o = (lax.axis_index(name) for name in names)
     low_bit = lax.rem(me_a, 2)
     partner = me_a + 1 - 2 * low_bit
@@ -170,6 +176,8 @@
         stacked = stacked + mm(chosen, patches[i].reshape(cols * levels, patches.shape[-1]))
     stacked = stacked.astype(BF16)
     load.wait()
+    for f in fetch:
+        f.start()
     embedded = mm(stacked, wbuf[...]) + level_embed[...]
     for band in range(levels):
         part = embedded[band * tile_rows : (band + 1) * tile_rows]
@@ -200,23 +208,17 @@
     own.wait()
     for copy in copies:
         copy.wait()
+    for f in fetch:
+        f.wait()
 
 
 def main_kernel(
     plan, names, sizes, wide, info, row_code, win, hm, lq, cross_gain, swin_gain, mlp_gain,
     cross_kv, cross_query, cross_out, swin_qkv, swin_out, mlp_up, mlp_down,
-    out,
-    b_kv, b_query, b_out, b_qkv, b_so, b_up, b_down, start, sems,
+    out, start,
 ):
     levels, _, lon_count = sizes
-    pairs = [
-        (cross_query, b_query), (cross_kv, b_kv), (cross_out, b_out), (swin_qkv, b_qkv),
-        (swin_out, b_so), (mlp_up, b_up), (mlp_down, b_down),
-    ]
-    loads = [pltpu.make_async_copy(a, b, sems.at[k]) for k, (a, b) in enumerate(pairs)]
-    for load in loads:
-        load.start()
-    l_query, l_kv, l_out, l_qkv, l_so, l_up, l_down = loads
+    b_kv, b_query, b_out, b_qkv, b_so, b_up, b_down = cross_kv, cross_query, cross_out, swin_qkv, swin_out, mlp_up, mlp_down
     me_l, me_o = lax.axis_index(names[0]), lax.axis_index(names[2])
     width = lq.shape[1]
     head_dim = width // HEADS
@@ -231,12 +233,10 @@
     meta_rows = [first + BLOCK - 1 for first, _ in plan.tiles]
 
     lq_f = lq[...].astype(F32)
-    l_query.wait()
     cq = (mm(lq[...], b_query[...]) * inv_root).astype(BF16).astype(F32)
     hm_f = hm[...].astype(F32)
     masked = jnp.concatenate([cq[q : q + 1] * hm_f for q in range(latents)], axis=0).astype(BF16)
 
-    l_kv.wait()
     keys, values, presence = [], [], []
     for level in range(levels):
         tokens = wide[level].astype(F32)
@@ -281,8 +281,6 @@
     weights = [(e / norm).astype(BF16) for e in exps]
     hm_all = jnp.concatenate([hm_f] * latents, axis=0)
     hm_row = lax.broadcasted_iota(jnp.int32, hm_all.shape, 0)
-    l_out.wait()
-    l_qkv.wait()
     queries, wkeys, wvalues = [], [], []
     for q in range(latents):
         expand = jnp.where(
@@ -328,11 +326,8 @@
                 piece = jnp.where(lane_head[h], total[h * own : (h + 1) * own], piece)
             pieces.append(piece)
         mixes.append(jnp.concatenate(pieces, axis=1))
-    l_so.wait()
     attended = start[...] + mm(jnp.concatenate(mixes, axis=0).astype(BF16), b_so[...])
     mlp_in = layer_norm(attended, mlp_gain[...]).astype(BF16)
-    l_up.wait()
-    l_down.wait()
     hidden = mlp_up.shape[1]
     result = attended
     step = 512
@@ -356,11 +351,14 @@
     vmem = pl.BlockSpec(memory_space=pltpu.VMEM)
     hbm = pl.BlockSpec(memory_space=pl.ANY)
     moves = 6 * levels - 1
-    wide = pl.pallas_call(
+    latents = latent_queries.shape[0]
+    weights = (cross_kv, cross_query, cross_out, swin_qkv, swin_out, mlp_up, mlp_down)
+    handed = 2 * (levels * plan.wide_rows * width + sum(w.size for w in weights))
+    wide, *weights = pl.pallas_call(
         functools.partial(send_kernel, plan, names, sizes),
-        out_shape=jax.ShapeDtypeStruct((levels, plan.wide_rows, width), BF16),
-        in_specs=[vmem, vmem, hbm, pl.BlockSpec(memory_space=pltpu.SMEM), vmem],
-        out_specs=vmem,
+        out_shape=[pltpu.VMEM((levels, plan.wide_rows, width), BF16)] + [pltpu.VMEM(w.shape, BF16) for w in weights],
+        in_specs=[vmem, vmem, hbm, pl.BlockSpec(memory_space=pltpu.SMEM), vmem] + [hbm] * 7,
+        out_specs=[vmem] * 8,
         scratch_shapes=[
             pltpu.VMEM(embed_weight.shape, BF16),
             pltpu.VMEM((bands, plan.tile_rows, width), BF16),
@@ -368,24 +366,23 @@
             pltpu.SemaphoreType.DMA((moves,)),
             pltpu.SemaphoreType.DMA((moves,)),
             pltpu.SemaphoreType.DMA,
+            pltpu.SemaphoreType.DMA((7,)),
         ],
-        compiler_params=pltpu.CompilerParams(collective_id=0, has_side_effects=True),
+        compiler_params=pltpu.CompilerParams(collective_id=0, has_side_effects=True, vmem_limit_bytes=VMEM - handed),
         name="send",
-    )(patches[0].transpose(1, 2, 0, 3), level_embed, embed_weight, block_ids, region_ids)
-    latents = latent_queries.shape[0]
+    )(patches[0].transpose(1, 2, 0, 3), level_embed, embed_weight, block_ids, region_ids, *weights)
     head_mask = (np.arange(width)[None, :] // (width // HEADS) == np.arange(HEADS)[:, None])
-    weights = (cross_kv, cross_query, cross_out, swin_qkv, swin_out, mlp_up, mlp_down)
+    weights = [pltpu.with_memory_space_constraint(w, pltpu.VMEM) for w in weights]
     tokens = pl.pallas_call(
         functools.partial(main_kernel, plan, names, sizes),
         out_shape=jax.ShapeDtypeStruct((plan.own, latents, width), F32),
-        in_specs=[vmem] * 9 + [hbm] * 7,
+        in_specs=[vmem] * 16,
         out_specs=vmem,
-        scratch_shapes=[pltpu.VMEM(w.shape, BF16) for w in weights]
-        + [pltpu.VMEM((latents * plan.own, width), F32), pltpu.SemaphoreType.DMA((7,))],
-        compiler_params=pltpu.CompilerParams(vmem_limit_bytes=56 << 20),
+        scratch_shapes=[pltpu.VMEM((latents * plan.own, width), F32)],
+        compiler_params=pltpu.CompilerParams(vmem_limit_bytes=40 << 20),
         name="main",
     )(
-        wide, jnp.asarray(plan.info), jnp.asarray(plan.row_code), jnp.asarray(plan.win),
+        pltpu.with_memory_space_constraint(wide, pltpu.VMEM), jnp.asarray(plan.info), jnp.asarray(plan.row_code), jnp.asarray(plan.win),
         jnp.asarray(head_mask, BF16), latent_queries, cross_gain.reshape(1, -1),
         swin_gain.reshape(1, -1), mlp_gain.reshape(1, -1), *weights,
     )

time: 25.6 us -> 22.3 us (0.87)
  Pallas kernels: 25.4 us -> 22 us
    pallas_call x1, Pallas kernels: 13.4 us -> 10.5 us  [shards(): pl.pallas_call(functools.partial(main_kernel, plan, names, sizes), out_sh...]
    pallas_call x1, Pallas kernels: 12 us -> 11.5 us  [shards(): pl.pallas_call(functools.partial(send_kernel, plan, names, sizes), out_sh...]
where the time goes in v1:
time: 22.3 us; the launch traced here: 22.1 us
  Pallas kernels  22 us (99%)
    pallas_call x1, Pallas kernels, shards(): pl.pallas_call(functools.partial(send_kernel, plan, names, sizes), out_sh...  11.5 us
    pallas_call x1, Pallas kernels, shards(): pl.pallas_call(functools.partial(main_kernel, plan, names, sizes), out_sh...  10.5 us

profile of v1, /device:TPU:0, one launch (start us, length us, event | category | flops | bytes accessed | tf_op | source)
XLA Modules:
  0.0 22.1 jit_solution(12419145502418828626)
XLA Ops:
  0.0 0.0 copy-start
  0.0 0.0 copy-start.1
  0.0 0.0 copy-start.2
  0.0 0.0 copy-start.3
  0.0 0.0 copy-start.4
  0.0 0.0 copy-start.5
  0.0 0.0 copy-start.6
  0.0 0.0 copy-start.7
  0.0 11.5 %send.1 = (bf16[2,160,512]{2,1,0:T(8,128)(2,1)S(1)}, bf16[512,1024]{1,0:T(8,128)(2,1)S(1)}, bf16[512,512]{1,0:T(8,128)(2,1)S(1)}, bf16[512,512]{1,0:T(8,128)(2,1...) custom-call(bf16[6,12,2,1000]{3,2,1,0:T(2,128)(2,1)} %bitcast.12, ...), custom_call_target="tpu_custom_call" | custom-call | tf_op jit(solution)/shard_map/send/pallas_call | solution.py:357
  11.6 0.0 copy-done
  11.6 0.0 copy-done.1
  11.6 0.0 copy-done.2
  11.6 0.0 copy-done.3
  11.6 0.0 copy-done.4
  11.6 0.0 copy-done.5
  11.6 0.0 copy-done.6
  11.6 0.0 copy-done.7
  11.6 10.5 %main.1 = f32[72,4,512]{2,1,0:T(4,128)} custom-call(bf16[2,160,512]{2,1,0:T(8,128)(2,1)S(1)} %get-tuple-element.13.wide, s32[216,128]{1,0:T(8,128)S(1)} %copy-done, s32[8,256]{1,0:T(8,128)S(1)} %copy-done.3, f32[72,216]{1,0:T(8,128)S(1)} %copy-done.1, bf16[16,512]{1,0:T(8,128)(2,1)S(1)} %copy-done.2, bf16[4,512]{1,0:T(4,128)(2,1)S(1)} %copy-done.4, ...), custom_call_target="tpu_custom_call" | custom-call | tf_op jit(solution)/shard_map/main/pallas_call | solution.py:376
Async XLA Ops:
  0.0 11.6 %copy-start = (s32[216,128]{1,0:T(8,128)S(1)}, s32[216,128]{1,0:T(8,128)}, u32[]{:S(2)}) copy-start(s32[216,128]{1,0:T(8,128)} %constant.8.clone.info) | copy-start | bytes 331780
  0.0 11.6 %copy-start.1 = (f32[72,216]{1,0:T(8,128)S(1)}, f32[72,216]{1,0:T(8,128)}, u32[]{:S(2)}) copy-start(f32[72,216]{1,0:T(8,128)} %constant.10.clone.win) | copy-start | bytes 186628
  0.0 11.6 %copy-start.2 = (bf16[16,512]{1,0:T(8,128)(2,1)S(1)}, bf16[16,512]{1,0:T(8,128)(2,1)}, u32[]{:S(2)}) copy-start(bf16[16,512]{1,0:T(8,128)(2,1)} %constant.11.clone.hm) | copy-start | bytes 49156
  0.0 11.6 %copy-start.3 = (s32[8,256]{1,0:T(8,128)S(1)}, s32[8,256]{1,0:T(8,128)}, u32[]{:S(2)}) copy-start(s32[8,256]{1,0:T(8,128)} %constant.9.clone.row_code) | copy-start | bytes 24580
  0.0 11.6 %copy-start.4 = (bf16[4,512]{1,0:T(4,128)(2,1)S(1)}, bf16[4,512]{1,0:T(4,128)(2,1)}, u32[]{:S(2)}) copy-start(bf16[4,512]{1,0:T(4,128)(2,1)} %lq.1) | copy-start | bytes 12292
  0.0 11.6 %copy-start.5 = (f32[512]{0:T(512)S(1)}, f32[512]{0:T(512)}, u32[]{:S(2)}) copy-start(f32[512]{0:T(512)} %param.25) | copy-start | bytes 6148
  0.0 11.6 %copy-start.6 = (f32[512]{0:T(512)S(1)}, f32[512]{0:T(512)}, u32[]{:S(2)}) copy-start(f32[512]{0:T(512)} %param.30) | copy-start | bytes 6148
  0.0 11.6 %copy-start.7 = (f32[512]{0:T(512)S(1)}, f32[512]{0:T(512)}, u32[]{:S(2)}) copy-start(f32[512]{0:T(512)} %param.33) | copy-start | bytes 6148

commit v2 on v1

v2 whole, which is shorter than its diff:
```python
import functools
import math

import jax
import jax.numpy as jnp
import numpy as np
from jax import lax
from jax.experimental import pallas as pl
from jax.experimental.pallas import tpu as pltpu
from jax.sharding import PartitionSpec as P

HEADS = 16
WIN_LAT = 6
BLOCK = 16
CODE = 64
LANES = 128
VMEM = 63700000
MESH = pl.DeviceIdType.MESH
F32 = jnp.float32
BF16 = jnp.bfloat16


def layer_norm(tensor, gain_vec):
    average = jnp.mean(tensor, axis=-1, keepdims=True)
    centred = tensor - average
    spread = jnp.mean(centred * centred, axis=-1, keepdims=True)
    return centred * lax.rsqrt(spread + 1e-05) * gain_vec


def mm(a, b):
    return jnp.dot(a, b, preferred_element_type=F32)


def mm_nt(a, b):
    return lax.dot_general(a, b, (((1,), (1,)), ((), ())), preferred_element_type=F32)


def add_all(parts):
    total = parts[0]
    for part in parts[1:]:
        total = total + part
    return total


def span(low, high, total, unit):
    first = low // 8 * 8
    size = -(-(high - first) // unit) * unit
    return min(first, total - size), size


class Plan:
    def __init__(self, rows, cols, cap, levels):
        self.rows, self.cols, self.cap, self.levels = rows, cols, cap, levels
        m = self.margin = WIN_LAT // 2
        per = (BLOCK - 1) // cap
        assert per >= m and rows < CODE and rows * cols <= LANES and cols == 2 * WIN_LAT
        groups = [list(range(per))]
        groups += [list(range(c, min(c + per, cols - per))) for c in range(per, cols - per, per)]
        groups += [list(range(cols - per, cols))]
        self.blocks = len(groups)
        self.tile_rows = self.blocks * BLOCK
        col_of = np.full((self.blocks, BLOCK), -1)
        for b, group in enumerate(groups):
            for k, c in enumerate(group):
                col_of[b, k * cap : (k + 1) * cap] = c
        self.col_of = col_of.reshape(-1)
        self.tiles = [(0, self.tile_rows), (self.tile_rows, self.tile_rows)]
        self.tiles += [(2 * self.tile_rows + k * BLOCK, BLOCK) for k in range(4)]
        self.wide_rows = 2 * self.tile_rows + 4 * BLOCK
        depth = min(levels, levels * cap - rows + 1)
        self.planes = [list(range(levels))] if depth == 1 else [[l] for l in range(levels)]
        share = len(self.planes[0])
        self.parts = [[0], [1], [2, 3, 4, 5]]
        first, last = self.col_of[:BLOCK], self.col_of[-BLOCK:]
        cols_of_tile = [self.col_of, self.col_of, last, last, first, first]
        self.row_code = np.full((8, LANES), -100000, np.int32)
        for g, part in enumerate(self.parts):
            codes = [
                np.where(cols_of_tile[t] >= 0, (k * cols + cols_of_tile[t]) * CODE, -100000)
                for k, t in enumerate(part)
            ]
            codes = np.concatenate(codes * share)
            assert len(codes) <= LANES
            self.row_code[g, : len(codes)] = codes
        edges = [0, m, cols - m, cols]
        spans = [range(edges[w], edges[w + 1]) for w in range(3)]
        own = [(i, j, w) for w in range(3) for i in range(rows) for j in spans[w]]
        self.own_cells = own
        self.own = n = rows * cols
        bounds = np.cumsum([0] + [rows * len(s) for s in spans])
        self.bounds = [int(b) for b in bounds]
        cells = [(t, 0, i, j) for t in (0, 1) for i, j, _ in own]
        halo = [spans[2], spans[2], spans[0], spans[0]]
        cells += [(2 + k, k, i, j) for k in range(4) for i in range(rows) for j in halo[k]]
        self.count = len(cells)
        assert self.count == 3 * n and n % 8 == 0
        self.info = np.full((self.count, LANES), -1, np.int32)
        t, k, i, j = np.array(cells).T
        self.info[:, 0] = (k * cols + j) * CODE + i
        self.info[:, 1] = i * cols + j
        self.info[:, 2] = t
        self.q_spans = [span(bounds[w], bounds[w + 1], n, 8) for w in range(3)]
        self.slots = [[], [], []]
        half = 2 * rows * m
        ranges = {0: [(w, bounds[w], bounds[w + 1]) for w in range(3)]}
        ranges[1] = ranges[0]
        ranges[2] = [(0, 0, half), (2, half, 2 * half)]
        self.used = [0, 0, 0]
        for g in range(3):
            for w, low, high in ranges[g]:
                low, high = int(low), int(high)
                first, size = (int(x) for x in span(low, high, n, 16))
                base = self.used[w]
                self.slots[g].append((w, first, size, base))
                self.info[g * n + low : g * n + high, 3 + w] = base + np.arange(low, high) - first
                self.used[w] += size
        assert max(self.used) <= LANES


def front_kernel(
    plan, names, sizes,
    patches, weight, level_embed, ids, labels, lq, cross_gain, swin_gain, info_in, code_in, hm_in,
    cross_query, cross_kv, cross_out, swin_qkv, swin_out, mlp_up, mlp_down,
    start, queries, kw, vw, mask, o_so, o_up, o_down,
    pbuf, wbuf, lebuf, idbuf, labbuf, lqbuf, cgain, sgain, info, codes, hm,
    b_query, b_kv, b_out, b_qkv, buf, wide, kq, ebuf, sems, send, recv,
):
    rows, cols, cap = plan.rows, plan.cols, plan.cap
    levels, lat_count, lon_count = sizes
    bands = levels
    width = weight.shape[1]
    latents = lq.shape[0]
    head_dim = width // HEADS
    inv_root = 1.0 / math.sqrt(head_dim)
    tile_rows = plan.tile_rows
    n = plan.own

    pairs = [
        (ids, idbuf), (labels, labbuf), (patches, pbuf), (weight, wbuf), (level_embed, lebuf),
        (lq, lqbuf), (cross_gain, cgain), (swin_gain, sgain), (info_in, info), (code_in, codes),
        (hm_in, hm), (cross_query, b_query), (cross_kv, b_kv), (cross_out, b_out),
        (swin_qkv, b_qkv), (swin_out, o_so), (mlp_up, o_up), (mlp_down, o_down),
    ]
    loads = [pltpu.make_async_copy(a, b, sems.at[k]) for k, (a, b) in enumerate(pairs)]
    for load in loads[:5]:
        load.start()

    me_l, me_a, me_o = (lax.axis_index(name) for name in names)
    partner = me_a + 1 - 2 * lax.rem(me_a, 2)
    lats = (me_a, partner)
    lons = {
        0: me_o,
        1: lax.rem(me_o + 1, lon_count),
        -1: lax.rem(me_o + lon_count - 1, lon_count),
    }
    band_of = [lax.rem(me_l + dm, levels) for dm in range(levels)]
    moves = [(dm, 0, 0) for dm in range(1, levels)]
    moves += [(dm, 1, 0) for dm in list(range(1, levels)) + [0]]
    moves += [(dm, da, do) for dm in list(range(1, levels)) + [0] for da in (1, 0) for do in (-1, 1)]
    barrier = pltpu.get_barrier_semaphore()
    for dm, da, do in moves:
        pl.semaphore_signal(
            barrier, inc=1, device_id=(band_of[dm], lats[da], lons[do]), device_id_type=MESH
        )

    row = lax.broadcasted_iota(jnp.int32, (tile_rows, 1), 0)
    in_block = jnp.bitwise_and(row, BLOCK - 1)
    col_step = add_all([(in_block >= k * cap).astype(jnp.int32) for k in range(1, BLOCK // cap + 1)])
    slot_of = in_block - col_step * cap
    col_of = jnp.zeros((tile_rows, 1), jnp.int32)
    used = jnp.zeros((tile_rows, 1), jnp.bool_)
    for b in range(plan.blocks):
        here = plan.col_of[b * BLOCK : (b + 1) * BLOCK]
        inside = (row >= b * BLOCK) & (row < (b + 1) * BLOCK)
        col_of = jnp.where(inside, int(here[0]) + col_step, col_of)
        used = used | ((row >= b * BLOCK) & (row < b * BLOCK + int((here >= 0).sum())))
    lane = lax.broadcasted_iota(jnp.int32, (1, LANES), 1)
    lane_in = jnp.bitwise_and(lane, BLOCK - 1)
    lane_step = add_all([(lane_in >= k * cap).astype(jnp.int32) for k in range(1, BLOCK // cap + 1)])
    lane_slot = lane_in - lane_step * cap
    cell = lax.broadcasted_iota(jnp.int32, (LANES, 1), 0)
    cell_i = add_all([(cell >= k * cols).astype(jnp.int32) for k in range(1, rows)])
    cell_j = cell - cell_i * cols
    picked_j = lax.broadcasted_iota(jnp.int32, (LANES, cols), 1) == cell_j
    eye = lax.broadcasted_iota(jnp.int32, (LANES, LANES), 0) == lax.broadcasted_iota(
        jnp.int32, (LANES, LANES), 1
    )
    loads[0].wait()
    loads[1].wait()
    lab = labbuf[...].astype(F32)
    col_lab = jnp.zeros((LANES, cols), F32)
    for k in range(rows):
        col_lab = jnp.where(cell_i == k, lab[k : k + 1, :], col_lab)
    lab_col = jnp.sum(jnp.where(picked_j, col_lab, 0.0), axis=1, keepdims=True)
    lab_row = jnp.sum(jnp.where(eye, lab_col, 0.0), axis=0, keepdims=True)
    picks, metas = [], []
    cells_all = rows * cols * bands
    source = lax.broadcasted_iota(jnp.int32, (tile_rows, cells_all), 1)
    for band in range(bands):
        id_col = jnp.full((tile_rows, 1), -1, jnp.int32)
        id_row = jnp.full((1, LANES), -1, jnp.int32)
        for s in range(cap):
            number = idbuf[0, band, 0, 0, s]
            id_col = jnp.where(slot_of == s, number, id_col)
            id_row = jnp.where(lane_slot == s, number, id_row)
        wanted = jnp.where(used & (id_col >= 0), (id_col * cols + col_of) * bands + band, -1)
        picks.append(jnp.where(source == wanted, 1.0, 0.0))
        pad = jnp.zeros((1, width - 2 * LANES), F32)
        metas.append(jnp.concatenate([id_row.astype(F32), lab_row, pad], axis=1))
    pick = jnp.concatenate(picks, axis=0).astype(BF16)
    loads[2].wait()
    cells_in = pbuf[...].reshape(cells_all, patches.shape[-1])
    loads[3].wait()
    for load in loads[5:]:
        load.start()
    loads[4].wait()
    embedded = (mm(cells_in, wbuf[...]) + lebuf[...]).astype(BF16)
    listed = mm(pick, embedded)
    for band in range(bands):
        part = listed[band * tile_rows : (band + 1) * tile_rows]
        buf[band] = jnp.where(in_block == BLOCK - 1, metas[band], part).astype(BF16)
    pl.semaphore_wait(barrier, len(moves))
    copies = {}
    for k, (dm, da, do) in enumerate(moves):
        if do == 0:
            origin, target, size = 0, plan.tiles[da][0], tile_rows
        elif do == 1:
            origin, target, size = tile_rows - BLOCK, plan.tiles[2 + da][0], BLOCK
        else:
            origin, target, size = 0, plan.tiles[4 + da][0], BLOCK
        copies[dm, da, do] = pltpu.make_async_remote_copy(
            src_ref=buf.at[band_of[dm], pl.ds(origin, size)],
            dst_ref=wide.at[me_l, pl.ds(target, size)],
            send_sem=send.at[k],
            recv_sem=recv.at[k],
            device_id=(band_of[dm], lats[da], lons[do]),
            device_id_type=MESH,
        )
        copies[dm, da, do].start()
    wide[me_l, pl.ds(0, tile_rows)] = buf[me_l]

    for w in range(3):
        for p in range(latents):
            if plan.used[w] < LANES:
                fill = jnp.zeros((LANES - plan.used[w], width), BF16)
                kw[w, p, plan.used[w] :] = fill
                vw[w, p, plan.used[w] :] = fill
    for load in loads[5:11]:
        load.wait()
    lq_f = lqbuf[...].astype(F32)
    hm_f = hm[...].astype(F32)
    hm_all = jnp.concatenate([hm_f] * latents, axis=0)
    hm_row = lax.broadcasted_iota(jnp.int32, hm_all.shape, 0)
    for q in range(latents):
        ebuf[:, q * width : (q + 1) * width] = jnp.where(
            (hm_row >= q * HEADS) & (hm_row < (q + 1) * HEADS), hm_all, 0.0
        ).astype(BF16)
    loads[11].wait()
    cq = (mm(lqbuf[...], b_query[...]) * inv_root).astype(BF16).astype(F32)
    masked = jnp.concatenate([cq[q : q + 1] * hm_f for q in range(latents)], axis=0).astype(BF16)
    loads[12].wait()
    kq[...] = mm_nt(b_kv[:, :width], masked).astype(BF16)
    loads[13].wait()
    loads[14].wait()

    def group_latents(g):
        part = plan.parts[g]
        code_c = info[g * n : (g + 1) * n, 0:1]
        low = plan.tiles[part[0]][0]
        size = sum(plan.tiles[t][1] for t in part)
        exps, values = [], []
        for plane in plan.planes:
            tokens = jnp.concatenate([wide[l, low : low + size] for l in plane], axis=0)
            id_row = jnp.full((1, LANES), -1.0, F32)
            begin = 0
            for l in plane:
                for t in part:
                    meta = plan.tiles[t][0]
                    line = wide[l, meta : meta + BLOCK, :LANES].astype(F32)[BLOCK - 1 :]
                    id_row = jnp.where(lane >= begin, line, id_row)
                    begin += plan.tiles[t][1]
            id_row = id_row.astype(jnp.int32)
            code_r = jnp.where(id_row >= 0, codes[g : g + 1, :] + id_row, -1)
            pick = jnp.where(code_c == code_r, 1.0, 0.0)[:, :begin]
            keys_in = layer_norm(mm(pick.astype(BF16), tokens), cgain[...]).astype(BF16)
            present = jnp.sum(pick, axis=1, keepdims=True)
            values.append(mm(keys_in, b_kv[:, width:]))
            exps.append(jnp.exp(mm(keys_in, kq[...])) * present)
        norm = add_all(exps)
        mixes = []
        for e, v in zip(exps, values):
            spread = mm((e / norm).astype(BF16), ebuf[...])
            mixes.append(
                jnp.concatenate(
                    [spread[:, q * width : (q + 1) * width] * v for q in range(latents)], axis=0
                )
            )
        out = mm(add_all(mixes).astype(BF16), b_out[...])
        latent = jnp.concatenate(
            [out[q * n : (q + 1) * n] + lq_f[q : q + 1] for q in range(latents)], axis=0
        )
        return latent, layer_norm(latent, sgain[...]).astype(BF16)

    def put(g, keys, values):
        for p in range(latents):
            for w, first, size, base in plan.slots[g]:
                cut = slice(p * n + first, p * n + first + size)
                kw[w, p, base : base + size] = keys[cut].astype(BF16)
                vw[w, p, base : base + size] = values[cut].astype(BF16)

    for move in moves:
        if move[1:] == (0, 0):
            copies[move].wait_recv()
    latent, normed = group_latents(0)
    start[...] = latent
    queries[...] = mm(normed, b_qkv[:, :width]) * inv_root
    put(0, mm(normed, b_qkv[:, width : 2 * width]), mm(normed, b_qkv[:, 2 * width :]))
    for move in moves:
        if move[1:] == (1, 0):
            copies[move].wait_recv()
    _, normed = group_latents(1)
    put(1, mm(normed, b_qkv[:, width : 2 * width]), mm(normed, b_qkv[:, 2 * width :]))
    for move in moves:
        if move[2] != 0:
            copies[move].wait_recv()
    _, normed = group_latents(2)
    put(2, mm(normed, b_qkv[:, width : 2 * width]), mm(normed, b_qkv[:, 2 * width :]))

    tile_c = info[:, 2:3]
    seg = jnp.zeros((plan.count, LANES), F32)
    for t, (first, _) in enumerate(plan.tiles):
        line = wide[me_l, first : first + BLOCK, LANES : 2 * LANES].astype(F32)[BLOCK - 1 :]
        seg = jnp.where(tile_c == t, line, seg)
    lab_col = jnp.sum(jnp.where(lane == info[:, 1:2], seg, 0.0), axis=1, keepdims=True)
    outside = ((tile_c >= 2) & (tile_c < 4) & (me_o == 0)) | ((tile_c >= 4) & (me_o == lon_count - 1))
    lab_key = jnp.where(outside, -1.0, lab_col)
    at = 0
    for w, (first, size) in enumerate(plan.q_spans):
        keys = jnp.where(lane == info[:, 3 + w : 4 + w], lab_key + 1.0, 0.0)
        keys = jnp.sum(keys, axis=0, keepdims=True) - 1.0
        mask[at : at + size] = jnp.where(lab_col[first : first + size] == keys, 1.0, 0.0)
        at += size

    for copy in copies.values():
        copy.wait_send()
    for load in loads[15:]:
        load.wait()


def back_kernel(plan, start, queries, kw, vw, mask, gain, b_so, b_up, b_down, out, obuf, sems):
    width = b_so.shape[0]
    head_dim = width // HEADS
    n = plan.own
    latents = start.shape[0] // n
    group = LANES // head_dim
    lane = lax.broadcasted_iota(jnp.int32, (1, LANES), 1)
    lane_head = [(lane >= h * head_dim) & (lane < (h + 1) * head_dim) for h in range(group)]
    low_half = lane < LANES // 2
    odd = add_all([jnp.where(lane_head[h], 1.0, 0.0) for h in range(1, group, 2)])
    halves = [(1.0 - odd).astype(BF16), odd.astype(BF16)]
    masks, at = [], 0
    for first, size in plan.q_spans:
        masks.append(mask[at : at + size])
        at += size
    sets = {}
    for p in range(latents):
        sets.setdefault((p + 1) // 2, []).append(p)
    sets = list(sets.values())
    units = [(g, w) for g in range(width // LANES) for w in range(3)]
    found = {}

    def scores(g, w):
        cut = slice(g * LANES, (g + 1) * LANES)
        first, size = plan.q_spans[w]
        raised = []
        for members in sets:
            parts = [queries[p * n + first : p * n + first + size, cut] for p in members]
            base = jnp.concatenate(parts, axis=0)
            if len(members) == 2:
                stack = jnp.concatenate([jnp.where(h, base, 0.0) for h in lane_head], axis=0)
                keys = jnp.concatenate([kw[w, p, :, cut] for p in members], axis=0)
            else:
                stack = jnp.concatenate(
                    [jnp.where(low_half, base, 0.0), jnp.where(low_half, 0.0, base)], axis=0
                )
                keys = jnp.concatenate([kw[w, members[0], :, cut] * h for h in halves], axis=0)
            raised.append(mm_nt(stack.astype(BF16), keys))
        return raised

    def mixed(g, w, raised):
        cut = slice(g * LANES, (g + 1) * LANES)
        first, size = plan.q_spans[w]
        weights = []
        for members, score in zip(sets, raised):
            allowed = jnp.concatenate([masks[w]] * (score.shape[0] // size), axis=0) > 0.5
            left = jnp.where(allowed, jnp.exp(score[:, :LANES]), 0.0)
            right = jnp.where(allowed, jnp.exp(score[:, LANES:]), 0.0)
            if len(members) == 2:
                inverse = 1.0 / jnp.sum(left + right, axis=1, keepdims=True)
                left, right = left * inverse, right * inverse
            else:
                left = left * (1.0 / jnp.sum(left, axis=1, keepdims=True))
                right = right * (1.0 / jnp.sum(right, axis=1, keepdims=True))
            weights.append(jnp.concatenate([left, right], axis=1).astype(BF16))
        for members, weight in zip(sets, weights):
            many = len(members) * size
            if len(members) == 2:
                values = jnp.concatenate([vw[w, p, :, cut] for p in members], axis=0)
                total = mm(weight, values)
                piece = total[:many]
                for h in range(1, group):
                    piece = jnp.where(lane_head[h], total[h * many : (h + 1) * many], piece)
            else:
                values = jnp.concatenate([vw[w, members[0], :, cut] * h for h in halves], axis=0)
                total = mm(weight, values)
                piece = jnp.where(low_half, total[:many], total[many:])
            for k, p in enumerate(members):
                found[p, g, w] = piece[k * size : (k + 1) * size]

    ahead = scores(*units[0])
    for k, unit in enumerate(units):
        now = ahead
        if k + 1 < len(units):
            ahead = scores(*units[k + 1])
        mixed(*unit, now)
    row = lax.broadcasted_iota(jnp.int32, (8, 1), 0)
    mixes = []
    for p in range(latents):
        columns = []
        for g in range(width // LANES):
            tiles = []
            for r in range(0, n, 8):
                tile = None
                for w, (first, size) in enumerate(plan.q_spans):
                    if plan.bounds[w] < r + 8 and plan.bounds[w + 1] > r:
                        here = found[p, g, w][r - first : r - first + 8]
                        tile = here if tile is None else jnp.where(row + r < plan.bounds[w], tile, here)
                tiles.append(tile)
            columns.append(jnp.concatenate(tiles, axis=0))
        mixes.append(jnp.concatenate(columns, axis=1))
    attended = start[...] + mm(jnp.concatenate(mixes, axis=0).astype(BF16), b_so[...])
    mlp_in = layer_norm(attended, gain[...]).astype(BF16)
    result = attended
    step = 512
    for c in range(0, b_up.shape[1], step):
        up = mm(mlp_in, b_up[:, c : c + step])
        act = (up * (1.0 + lax.erf(up * math.sqrt(0.5))) * 0.5).astype(BF16)
        result = result + mm(act, b_down[c : c + step, :])
    for p in range(latents):
        obuf[:, p, :] = result[p * n : (p + 1) * n]
    writes, k = [], 0
    while k < n:
        i, j, w = plan.own_cells[k]
        size = 1
        while k + size < n and plan.own_cells[k + size] == (i, j + size, w):
            size += 1
        target = i * plan.cols + j
        writes.append(
            pltpu.make_async_copy(
                obuf.at[pl.ds(k, size)], out.at[pl.ds(target, size)], sems.at[len(writes)]
            )
        )
        k += size
    for write in writes:
        write.start()
    for write in writes:
        write.wait()


def shards(
    sizes, names,
    patches, level_embed, embed_weight, block_ids, latent_queries, cross_gain, cross_query, cross_kv,
    cross_out, region_ids, swin_gain, swin_qkv, swin_out, mlp_gain, mlp_up, mlp_down,
):
    levels = sizes[0]
    _, bands, rows, cols, features = patches.shape
    assert bands == levels
    width = embed_weight.shape[1]
    latents = latent_queries.shape[0]
    plan = Plan(rows, cols, block_ids.shape[-1], levels)
    n = plan.own
    head_mask = np.arange(width)[None, :] // (width // HEADS) == np.arange(HEADS)[:, None]
    vmem = pl.BlockSpec(memory_space=pltpu.VMEM)
    hbm = pl.BlockSpec(memory_space=pl.ANY)
    moves = 6 * levels - 1
    q_rows = sum(size for _, size in plan.q_spans)
    handed = [
        ((latents * n, width), F32), ((latents * n, width), F32),
        ((3, latents, LANES, width), BF16), ((3, latents, LANES, width), BF16),
        ((q_rows, LANES), F32),
        (swin_out.shape, BF16), (mlp_up.shape, BF16), (mlp_down.shape, BF16),
    ]
    room = int(sum(math.prod(shape) * np.dtype(kind).itemsize for shape, kind in handed))
    inputs = (
        patches[0].transpose(1, 2, 0, 3), embed_weight, level_embed, block_ids, region_ids,
        latent_queries, cross_gain.reshape(1, -1), swin_gain.reshape(1, -1),
        jnp.asarray(plan.info), jnp.asarray(plan.row_code), jnp.asarray(head_mask, BF16),
    )
    weights = (cross_query, cross_kv, cross_out, swin_qkv)
    later = (swin_out, mlp_up, mlp_down)
    held = [pltpu.VMEM(x.shape, x.dtype) for x in inputs]
    held[3] = pltpu.SMEM(block_ids.shape, jnp.int32)
    order = (0, 1, 2, 3, 4, 5, 6, 7, 8, 9, 10)
    outs = pl.pallas_call(
        functools.partial(front_kernel, plan, names, sizes),
        out_shape=[pltpu.VMEM(shape, kind) for shape, kind in handed],
        in_specs=[hbm] * 18,
        out_specs=[vmem] * 8,
        scratch_shapes=[held[k] for k in order]
        + [pltpu.VMEM(w.shape, BF16) for w in weights]
        + [
            pltpu.VMEM((bands, plan.tile_rows, width), BF16),
            pltpu.VMEM((levels, plan.wide_rows, width), BF16),
            pltpu.VMEM((width, latents * HEADS), BF16),
            pltpu.VMEM((latents * HEADS, latents * width), BF16),
            pltpu.SemaphoreType.DMA((18,)),
            pltpu.SemaphoreType.DMA((moves,)),
            pltpu.SemaphoreType.DMA((moves,)),
        ],
        compiler_params=pltpu.CompilerParams(
            collective_id=0, has_side_effects=True, vmem_limit_bytes=VMEM - room
        ),
        name="front",
    )(*inputs, *weights, *later)
    outs = [pltpu.with_memory_space_constraint(x, pltpu.VMEM) for x in outs]
    tokens = pl.pallas_call(
        functools.partial(back_kernel, plan),
        out_shape=jax.ShapeDtypeStruct((n, latents, width), F32),
        in_specs=[vmem] * 9,
        out_specs=hbm,
        scratch_shapes=[
            pltpu.VMEM((n, latents, width), F32),
            pltpu.SemaphoreType.DMA((3 * rows,)),
        ],
        compiler_params=pltpu.CompilerParams(vmem_limit_bytes=40 << 20),
        name="back",
    )(*outs[:5], mlp_gain.reshape(1, -1), *outs[5:])
    return tokens.reshape(rows, cols, latents, width).transpose(2, 0, 1, 3)


def solution(mesh):
    names = ("lvl", "lat", "lon")
    sizes = tuple(mesh.shape[name] for name in names)
    tiled = P("lvl", None, "lat", "lon", None)
    return jax.shard_map(
        functools.partial(shards, sizes, names),
        mesh=mesh,
        in_specs=(
            tiled, P("lvl", None), P(), tiled, P(), P(), P(), P(), P(), P(("lvl", "lat"), "lon"),
            P(), P(), P(), P(), P(), P(),
        ),
        out_specs=P(None, ("lvl", "lat"), "lon", None),
        check_vma=False,
    )
```

time: 22.3 us -> 19.8 us (0.89)
  Pallas kernels: 22 us -> 19.6 us
    pallas_call x2, Pallas kernels: 22 us -> 19.6 us  [the longest x1 14.4 us: shards(): pl.pallas_call(functools.partial(front_kernel, plan, names, sizes), out_s...]
where the time goes in v2:
time: 19.8 us; the launch traced here: 19.6 us
  Pallas kernels  19.6 us (99%)
    pallas_call x1, Pallas kernels, shards(): pl.pallas_call(functools.partial(front_kernel, plan, names, sizes), out_s...  14.4 us
    pallas_call x1, Pallas kernels, shards(): pl.pallas_call(functools.partial(back_kernel, plan), out_shape=jax.ShapeD...  5.2 us

profile of v2, /device:TPU:0, one launch (start us, length us, event | category | flops | bytes accessed | tf_op | source)
XLA Modules:
  0.0 19.6 jit_solution(291369768310330438)
XLA Ops:
  0.0 0.0 copy-start
  0.0 14.4 %front.1 = (f32[288,512]{1,0:T(8,128)S(1)}, f32[288,512]{1,0:T(8,128)S(1)}, bf16[3,4,128,512]{3,2,1,0:T(8,128)(2,1)S(1)}, bf16[3,4,128,512]{3,2,1,0:T(8,128)(2,1...) custom-call(bf16[6,12,2,1000]{3,2,1,0:T(2,128)(2,1)} %bitcast.10, ...), custom_call_target="tpu_custom_call" | custom-call | tf_op jit(solution)/shard_map/front/pallas_call | solution.py:504
  14.4 0.0 copy-done
  14.4 5.2 %back.1 = f32[72,4,512]{2,1,0:T(4,128)} custom-call(f32[288,512]{1,0:T(8,128)S(1)} %get-tuple-element.13.start, f32[288,512]{1,0:T(8,128)S(1)} %get-tuple-element.14.queries, bf16[3,4,128,512]{3,2,1,0:T(8,128)(2,1)S(1)} %get-tuple-element.15.kw, bf16[3,4,128,512]{3,2,1,0:T(8,128)(2,1)S(1)} %get-tuple-element.16.vw, f32[88,128]{1,0:T(8,128)S(1)} %get-tuple-element.17.mask, ...), custom_call_target="tpu_custom_call" | custom-call | tf_op jit(solution)/shard_map/back/pallas_call | solution.py:526
Async XLA Ops:
  0.0 14.4 %copy-start = (f32[512]{0:T(512)S(1)}, f32[512]{0:T(512)}, u32[]{:S(2)}) copy-start(f32[512]{0:T(512)} %param.32) | copy-start | bytes 6148

commit v3 on v2

--- a/solution.py
+++ b/solution.py
@@ -154,14 +154,20 @@
         -1: lax.rem(me_o + lon_count - 1, lon_count),
     }
     band_of = [lax.rem(me_l + dm, levels) for dm in range(levels)]
-    moves = [(dm, 0, 0) for dm in range(1, levels)]
-    moves += [(dm, 1, 0) for dm in list(range(1, levels)) + [0]]
-    moves += [(dm, da, do) for dm in list(range(1, levels)) + [0] for da in (1, 0) for do in (-1, 1)]
+    direct = [(dm, 0) for dm in range(1, levels)] + [(dm, 1) for dm in range(levels)]
+    targets = [(band_of[dm], lats[da], me_o) for dm, da in direct]
+    sides = [(da, do) for da in (0, 1) for do in (1, -1)]
+    beside = {(da, do): (me_l, lats[da], lons[do]) for da, do in sides}
+    inner = {1: me_o < lon_count - 1, -1: me_o > 0}
     barrier = pltpu.get_barrier_semaphore()
-    for dm, da, do in moves:
-        pl.semaphore_signal(
-            barrier, inc=1, device_id=(band_of[dm], lats[da], lons[do]), device_id_type=MESH
-        )
+    for target in targets:
+        pl.semaphore_signal(barrier, inc=1, device_id=target, device_id_type=MESH)
+    for do in (1, -1):
+
+        @pl.when(inner[do])
+        def _():
+            for da in (0, 1):
+                pl.semaphore_signal(barrier, inc=1, device_id=beside[da, do], device_id_type=MESH)
 
     row = lax.broadcasted_iota(jnp.int32, (tile_rows, 1), 0)
     in_block = jnp.bitwise_and(row, BLOCK - 1)
@@ -219,25 +225,46 @@
     for band in range(bands):
         part = listed[band * tile_rows : (band + 1) * tile_rows]
         buf[band] = jnp.where(in_block == BLOCK - 1, metas[band], part).astype(BF16)
-    pl.semaphore_wait(barrier, len(moves))
+    pl.semaphore_wait(barrier, len(targets) + 2 * add_all([inner[do].astype(jnp.int32) for do in (1, -1)]))
     copies = {}
-    for k, (dm, da, do) in enumerate(moves):
-        if do == 0:
-            origin, target, size = 0, plan.tiles[da][0], tile_rows
-        elif do == 1:
-            origin, target, size = tile_rows - BLOCK, plan.tiles[2 + da][0], BLOCK
-        else:
-            origin, target, size = 0, plan.tiles[4 + da][0], BLOCK
-        copies[dm, da, do] = pltpu.make_async_remote_copy(
-            src_ref=buf.at[band_of[dm], pl.ds(origin, size)],
-            dst_ref=wide.at[me_l, pl.ds(target, size)],
+    for k, (dm, da) in enumerate(direct):
+        copies[dm, da] = pltpu.make_async_remote_copy(
+            src_ref=buf.at[band_of[dm]],
+            dst_ref=wide.at[me_l, pl.ds(plan.tiles[da][0], tile_rows)],
             send_sem=send.at[k],
             recv_sem=recv.at[k],
-            device_id=(band_of[dm], lats[da], lons[do]),
+            device_id=targets[k],
             device_id_type=MESH,
         )
-        copies[dm, da, do].start()
+    relays = {}
+    for dm in range(levels):
+        level = lax.rem(me_l + dm, levels)
+        for da, do in sides:
+            origin = tile_rows - BLOCK if do == 1 else 0
+            target = plan.tiles[(2 if do == 1 else 4) + da][0]
+            slot = len(direct) + len(relays)
+            relays[dm, da, do] = pltpu.make_async_remote_copy(
+                src_ref=(wide if dm else buf).at[level, pl.ds(origin, BLOCK)],
+                dst_ref=wide.at[level, pl.ds(target, BLOCK)],
+                send_sem=send.at[slot],
+                recv_sem=recv.at[slot],
+                device_id=beside[da, do],
+                device_id_type=MESH,
+            )
+    near = [move for move in direct if move[0] == 0 or move[1] == 0]
+    far = [move for move in direct if move not in near]
+    for move in near:
+        copies[move].start()
+    for da, do in sides:
+        pl.when(inner[do])(relays[0, da, do].start)
     wide[me_l, pl.ds(0, tile_rows)] = buf[me_l]
+    for side, (first, count) in ((-1, (2, 2)), (1, (4, 2))):
+
+        @pl.when(jnp.logical_not(inner[side]))
+        def _():
+            low = plan.tiles[first][0]
+            wide[:, low : low + count * BLOCK] = jnp.zeros((levels, count * BLOCK, width), BF16)
+
 
     for w in range(3):
         for p in range(latents):
@@ -245,6 +272,8 @@
                 fill = jnp.zeros((LANES - plan.used[w], width), BF16)
                 kw[w, p, plan.used[w] :] = fill
                 vw[w, p, plan.used[w] :] = fill
+    for move in far:
+        copies[move].start()
     for load in loads[5:11]:
         load.wait()
     lq_f = lqbuf[...].astype(F32)
@@ -263,7 +292,7 @@
     loads[13].wait()
     loads[14].wait()
 
-    def group_latents(g):
+    def head(g):
         part = plan.parts[g]
         code_c = info[g * n : (g + 1) * n, 0:1]
         low = plan.tiles[part[0]][0]
@@ -282,67 +311,101 @@
             id_row = id_row.astype(jnp.int32)
             code_r = jnp.where(id_row >= 0, codes[g : g + 1, :] + id_row, -1)
             pick = jnp.where(code_c == code_r, 1.0, 0.0)[:, :begin]
-            keys_in = layer_norm(mm(pick.astype(BF16), tokens), cgain[...]).astype(BF16)
+            found = mm(pick.astype(BF16), tokens)
+            yield
+            keys_in = layer_norm(found, cgain[...]).astype(BF16)
             present = jnp.sum(pick, axis=1, keepdims=True)
+            score = mm(keys_in, kq[...])
             values.append(mm(keys_in, b_kv[:, width:]))
-            exps.append(jnp.exp(mm(keys_in, kq[...])) * present)
+            yield
+            exps.append(jnp.exp(score) * present)
         norm = add_all(exps)
+        norm = jnp.where(norm > 0.0, norm, 1.0)
+        mixers[g] = [(e / norm).astype(BF16) for e in exps], values
+
+    def tail(g, picked):
+        weights, values = mixers[g]
+        low, high = picked[0] * width, (picked[-1] + 1) * width
+        spreads = [mm(weight, ebuf[:, low:high]) for weight in weights]
+        yield
         mixes = []
-        for e, v in zip(exps, values):
-            spread = mm((e / norm).astype(BF16), ebuf[...])
-            mixes.append(
-                jnp.concatenate(
-                    [spread[:, q * width : (q + 1) * width] * v for q in range(latents)], axis=0
-                )
-            )
+        for spread, v in zip(spreads, values):
+            cuts = [spread[:, k * width : (k + 1) * width] * v for k in range(len(picked))]
+            mixes.append(jnp.concatenate(cuts, axis=0))
         out = mm(add_all(mixes).astype(BF16), b_out[...])
+        yield
         latent = jnp.concatenate(
-            [out[q * n : (q + 1) * n] + lq_f[q : q + 1] for q in range(latents)], axis=0
+            [out[k * n : (k + 1) * n] + lq_f[p : p + 1] for k, p in enumerate(picked)], axis=0
         )
-        return latent, layer_norm(latent, sgain[...]).astype(BF16)
-
-    def put(g, keys, values):
-        for p in range(latents):
+        normed = layer_norm(latent, sgain[...]).astype(BF16)
+        if g == 0:
+            start[picked[0] * n : (picked[-1] + 1) * n] = latent
+            asked = mm(normed, b_qkv[:, :width])
+        keys = mm(normed, b_qkv[:, width : 2 * width])
+        values = mm(normed, b_qkv[:, 2 * width :])
+        yield
+        if g == 0:
+            queries[picked[0] * n : (picked[-1] + 1) * n] = asked * inv_root
+        for k, p in enumerate(picked):
             for w, first, size, base in plan.slots[g]:
-                cut = slice(p * n + first, p * n + first + size)
+                cut = slice(k * n + first, k * n + first + size)
                 kw[w, p, base : base + size] = keys[cut].astype(BF16)
                 vw[w, p, base : base + size] = values[cut].astype(BF16)
 
-    for move in moves:
-        if move[1:] == (0, 0):
+    def run(works):
+        works = [iter(work) for work in works]
+        waiting, live = list(works), []
+        while waiting or live:
+            if waiting:
+                live.append(waiting.pop(0))
+            for work in list(live):
+                if next(work, run) is run:
+                    live.remove(work)
+
+    def view():
+        tile_c = info[:, 2:3]
+        seg = jnp.zeros((plan.count, LANES), F32)
+        for t, (first, _) in enumerate(plan.tiles):
+            line = wide[me_l, first : first + BLOCK, LANES : 2 * LANES].astype(F32)[BLOCK - 1 :]
+            seg = jnp.where(tile_c == t, line, seg)
+        lab_col = jnp.sum(jnp.where(lane == info[:, 1:2], seg, 0.0), axis=1, keepdims=True)
+        yield
+        outside = (tile_c >= 2) & (tile_c < 4) & (me_o == 0)
+        outside = outside | ((tile_c >= 4) & (me_o == lon_count - 1))
+        lab_key = jnp.where(outside, -1.0, lab_col)
+        at = 0
+        for w, (first, size) in enumerate(plan.q_spans):
+            keys = jnp.where(lane == info[:, 3 + w : 4 + w], lab_key + 1.0, 0.0)
+            keys = jnp.sum(keys, axis=0, keepdims=True) - 1.0
+            mask[at : at + size] = jnp.where(lab_col[first : first + size] == keys, 1.0, 0.0)
+            at += size
+            yield
+
+    mixers = {}
+    half = -(-latents // 2)
+    halves = [list(range(latents))]
+    for move in direct:
+        if move[1] == 0:
             copies[move].wait_recv()
-    latent, normed = group_latents(0)
-    start[...] = latent
-    queries[...] = mm(normed, b_qkv[:, :width]) * inv_root
-    put(0, mm(normed, b_qkv[:, width : 2 * width]), mm(normed, b_qkv[:, 2 * width :]))
-    for move in moves:
-        if move[1:] == (1, 0):
+    for (dm, _, do), relay in relays.items():
+        if dm:
+            pl.when(inner[do])(relay.start)
+    run([head(0)])
+    run([tail(0, picked) for picked in halves])
+    for move in direct:
+        if move[1] == 1:
             copies[move].wait_recv()
-    _, normed = group_latents(1)
-    put(1, mm(normed, b_qkv[:, width : 2 * width]), mm(normed, b_qkv[:, 2 * width :]))
-    for move in moves:
-        if move[2] != 0:
-            copies[move].wait_recv()
-    _, normed = group_latents(2)
-    put(2, mm(normed, b_qkv[:, width : 2 * width]), mm(normed, b_qkv[:, 2 * width :]))
-
-    tile_c = info[:, 2:3]
-    seg = jnp.zeros((plan.count, LANES), F32)
-    for t, (first, _) in enumerate(plan.tiles):
-        line = wide[me_l, first : first + BLOCK, LANES : 2 * LANES].astype(F32)[BLOCK - 1 :]
-        seg = jnp.where(tile_c == t, line, seg)
-    lab_col = jnp.sum(jnp.where(lane == info[:, 1:2], seg, 0.0), axis=1, keepdims=True)
-    outside = ((tile_c >= 2) & (tile_c < 4) & (me_o == 0)) | ((tile_c >= 4) & (me_o == lon_count - 1))
-    lab_key = jnp.where(outside, -1.0, lab_col)
-    at = 0
-    for w, (first, size) in enumerate(plan.q_spans):
-        keys = jnp.where(lane == info[:, 3 + w : 4 + w], lab_key + 1.0, 0.0)
-        keys = jnp.sum(keys, axis=0, keepdims=True) - 1.0
-        mask[at : at + size] = jnp.where(lab_col[first : first + size] == keys, 1.0, 0.0)
-        at += size
+    run([head(1)])
+    run([tail(1, picked) for picked in halves])
+    for (_, _, do), relay in relays.items():
+        pl.when(inner[-do])(relay.wait_recv)
+    run([head(2), view()])
+    run([tail(2, picked) for picked in halves])
 
     for copy in copies.values():
         copy.wait_send()
+    for (_, _, do), relay in relays.items():
+        pl.when(inner[do])(relay.wait_send)
     for load in loads[15:]:
         load.wait()
 
@@ -417,37 +480,68 @@
             for k, p in enumerate(members):
                 found[p, g, w] = piece[k * size : (k + 1) * size]
 
+    row = lax.broadcasted_iota(jnp.int32, (8, 1), 0)
+
+    def merged(p, g):
+        tiles = []
+        for r in range(0, n, 8):
+            tile = None
+            for w, (first, size) in enumerate(plan.q_spans):
+                if plan.bounds[w] < r + 8 and plan.bounds[w + 1] > r:
+                    here = found[p, g, w][r - first : r - first + 8]
+                    tile = here if tile is None else jnp.where(row + r < plan.bounds[w], tile, here)
+            tiles.append(tile)
+        return jnp.concatenate(tiles, axis=0)
+
+    half = -(-latents // 2)
+    halves_of = [list(range(half)), list(range(half, latents))]
+    attended = {}
+
+    def project(low, high):
+        for k, picked in enumerate(halves_of):
+            mix = [[merged(p, g) for g in range(low, high)] for p in picked]
+            mix = jnp.concatenate([jnp.concatenate(m, axis=1) for m in mix], axis=0).astype(BF16)
+            base = attended[k] if low else start[picked[0] * n : (picked[-1] + 1) * n]
+            attended[k] = base + mm(mix, b_so[low * LANES : high * LANES])
+
+    results = {}
+    step = 512
+
+    def tail(picked):
+        k = halves_of.index(picked)
+        result = attended[k]
+        mlp_in = layer_norm(result, gain[...]).astype(BF16)
+        chunks = list(range(0, b_up.shape[1], step))
+        ahead = mm(mlp_in, b_up[:, :step])
+        yield
+        for c in chunks:
+            up = ahead
+            if c + step < b_up.shape[1]:
+                ahead = mm(mlp_in, b_up[:, c + step : c + 2 * step])
+            act = (up * (1.0 + lax.erf(up * math.sqrt(0.5))) * 0.5).astype(BF16)
+            result = result + mm(act, b_down[c : c + step, :])
+            yield
+        for m, p in enumerate(picked):
+            results[p] = result[m * n : (m + 1) * n]
+
+    middle = width // LANES // 2
     ahead = scores(*units[0])
     for k, unit in enumerate(units):
         now = ahead
         if k + 1 < len(units):
             ahead = scores(*units[k + 1])
         mixed(*unit, now)
-    row = lax.broadcasted_iota(jnp.int32, (8, 1), 0)
-    mixes = []
+    project(0, width // LANES)
+    works = [tail(picked) for picked in halves_of]
+    waiting, live = works, []
+    while waiting or live:
+        if waiting:
+            live.append(waiting.pop(0))
+        for work in list(live):
+            if next(work, works) is works:
+                live.remove(work)
     for p in range(latents):
-        columns = []
-        for g in range(width // LANES):
-            tiles = []
-            for r in range(0, n, 8):
-                tile = None
-                for w, (first, size) in enumerate(plan.q_spans):
-                    if plan.bounds[w] < r + 8 and plan.bounds[w + 1] > r:
-                        here = found[p, g, w][r - first : r - first + 8]
-                        tile = here if tile is None else jnp.where(row + r < plan.bounds[w], tile, here)
-                tiles.append(tile)
-            columns.append(jnp.concatenate(tiles, axis=0))
-        mixes.append(jnp.concatenate(columns, axis=1))
-    attended = start[...] + mm(jnp.concatenate(mixes, axis=0).astype(BF16), b_so[...])
-    mlp_in = layer_norm(attended, gain[...]).astype(BF16)
-    result = attended
-    step = 512
-    for c in range(0, b_up.shape[1], step):
-        up = mm(mlp_in, b_up[:, c : c + step])
-        act = (up * (1.0 + lax.erf(up * math.sqrt(0.5))) * 0.5).astype(BF16)
-        result = result + mm(act, b_down[c : c + step, :])
-    for p in range(latents):
-        obuf[:, p, :] = result[p * n : (p + 1) * n]
+        obuf[:, p, :] = results[p]
     writes, k = [], 0
     while k < n:
         i, j, w = plan.own_cells[k]

time: 19.8 us -> 18 us (0.909)
  Pallas kernels: 19.6 us -> 17.9 us
    pallas_call x1, Pallas kernels: 14.4 us -> 13 us  [shards(): pl.pallas_call(functools.partial(front_kernel, plan, names, sizes), out_s...]
    pallas_call x1, Pallas kernels: 5.2 us -> 4.86 us  [shards(): pl.pallas_call(functools.partial(back_kernel, plan), out_shape=jax.ShapeD...]
where the time goes in v3:
time: 18 us; the launch traced here: 17.9 us
  Pallas kernels  17.9 us (99%)
    pallas_call x1, Pallas kernels, shards(): pl.pallas_call(functools.partial(front_kernel, plan, names, sizes), out_s...  13 us
    pallas_call x1, Pallas kernels, shards(): pl.pallas_call(functools.partial(back_kernel, plan), out_shape=jax.ShapeD...  4.86 us

profile of v3, /device:TPU:0, one launch (start us, length us, event | category | flops | bytes accessed | tf_op | source)
XLA Modules:
  0.0 17.9 jit_solution(8981937114313424021)
XLA Ops:
  0.0 0.0 copy-start
  0.0 13.0 %front.1 = (f32[288,512]{1,0:T(8,128)S(1)}, f32[288,512]{1,0:T(8,128)S(1)}, bf16[3,4,128,512]{3,2,1,0:T(8,128)(2,1)S(1)}, bf16[3,4,128,512]{3,2,1,0:T(8,128)(2,1...) custom-call(bf16[6,12,2,1000]{3,2,1,0:T(2,128)(2,1)} %bitcast.10, ...), custom_call_target="tpu_custom_call" | custom-call | tf_op jit(solution)/shard_map/front/pallas_call | solution.py:598
  13.0 0.0 copy-done
  13.0 4.9 %back.1 = f32[72,4,512]{2,1,0:T(4,128)} custom-call(f32[288,512]{1,0:T(8,128)S(1)} %get-tuple-element.13.start, f32[288,512]{1,0:T(8,128)S(1)} %get-tuple-element.14.queries, bf16[3,4,128,512]{3,2,1,0:T(8,128)(2,1)S(1)} %get-tuple-element.15.kw, bf16[3,4,128,512]{3,2,1,0:T(8,128)(2,1)S(1)} %get-tuple-element.16.vw, f32[88,128]{1,0:T(8,128)S(1)} %get-tuple-element.17.mask, ...), custom_call_target="tpu_custom_call" | custom-call | tf_op jit(solution)/shard_map/back/pallas_call | solution.py:620
Async XLA Ops:
  0.0 13.0 %copy-start = (f32[512]{0:T(512)S(1)}, f32[512]{0:T(512)}, u32[]{:S(2)}) copy-start(f32[512]{0:T(512)} %param.32) | copy-start | bytes 6148

commit v4 on v3

v4 whole, which is shorter than its diff:
```python
import functools
import math

import jax
import jax.numpy as jnp
import numpy as np
from jax import lax
from jax.experimental import pallas as pl
from jax.experimental.pallas import tpu as pltpu
from jax.sharding import PartitionSpec as P

HEADS = 16
WIN_LAT = 6
BLOCK = 16
CODE = 64
KCUT = 256
AHEAD = 2
LANES = 128
VMEM = 63700000
MESH = pl.DeviceIdType.MESH
F32 = jnp.float32
BF16 = jnp.bfloat16


def layer_norm(tensor, gain_vec):
    average = jnp.mean(tensor, axis=-1, keepdims=True)
    centred = tensor - average
    spread = jnp.mean(centred * centred, axis=-1, keepdims=True)
    return centred * lax.rsqrt(spread + 1e-05) * gain_vec


def mm(a, b):
    return jnp.dot(a, b, preferred_element_type=F32)


def mm_nt(a, b):
    return lax.dot_general(a, b, (((1,), (1,)), ((), ())), preferred_element_type=F32)


def add_all(parts):
    total = parts[0]
    for part in parts[1:]:
        total = total + part
    return total


def span(low, high, total, unit):
    first = low // 8 * 8
    size = -(-(high - first) // unit) * unit
    return min(first, total - size), size


class Plan:
    def __init__(self, rows, cols, cap, levels):
        self.rows, self.cols, self.cap, self.levels = rows, cols, cap, levels
        m = self.margin = WIN_LAT // 2
        per = (BLOCK - 1) // cap
        assert per >= m and rows < CODE and rows * cols <= LANES and cols == 2 * WIN_LAT
        groups = [list(range(per))]
        groups += [list(range(c, min(c + per, cols - per))) for c in range(per, cols - per, per)]
        groups += [list(range(cols - per, cols))]
        sizes = [-(-len(group) * cap // 8) * 8 for group in groups]
        sizes[0] = sizes[-1] = BLOCK
        self.starts = [sum(sizes[:b]) for b in range(len(groups))]
        self.groups = groups
        self.tile_rows = sum(sizes)
        self.col_of = np.full(self.tile_rows, -1)
        for first, group in zip(self.starts, groups):
            for k, c in enumerate(group):
                self.col_of[first + k * cap : first + (k + 1) * cap] = c
        pitch = -(-self.tile_rows // BLOCK) * BLOCK
        self.tiles = [(0, self.tile_rows), (pitch, self.tile_rows)]
        self.tiles += [(2 * pitch + k * BLOCK, BLOCK) for k in range(4)]
        self.wide_rows = 2 * pitch + 4 * BLOCK
        depth = min(levels, levels * cap - rows + 1)
        self.planes = [list(range(levels))] if depth == 1 else [[l] for l in range(levels)]
        share = len(self.planes[0])
        self.parts = [[0], [1], [2, 3, 4, 5]]
        first, last = self.col_of[:BLOCK], self.col_of[-BLOCK:]
        cols_of_tile = [self.col_of, self.col_of, last, last, first, first]
        self.row_code = np.full((8, LANES), -100000, np.int32)
        for g, part in enumerate(self.parts):
            codes = [
                np.where(cols_of_tile[t] >= 0, (k * cols + cols_of_tile[t]) * CODE, -100000)
                for k, t in enumerate(part)
            ]
            codes = np.concatenate(codes * share)
            assert len(codes) <= LANES
            self.row_code[g, : len(codes)] = codes
        edges = [0, m, cols - m, cols]
        spans = [range(edges[w], edges[w + 1]) for w in range(3)]
        own = [(i, j, w) for w in range(3) for i in range(rows) for j in spans[w]]
        self.own_cells = own
        self.own = n = rows * cols
        bounds = np.cumsum([0] + [rows * len(s) for s in spans])
        self.bounds = [int(b) for b in bounds]
        cells = [(t, 0, i, j) for t in (0, 1) for i, j, _ in own]
        halo = [spans[2], spans[2], spans[0], spans[0]]
        cells += [(2 + k, k, i, j) for k in range(4) for i in range(rows) for j in halo[k]]
        self.count = len(cells)
        assert self.count == 3 * n and n % 8 == 0
        self.info = np.full((self.count, LANES), -1, np.int32)
        t, k, i, j = np.array(cells).T
        self.info[:, 0] = (k * cols + j) * CODE + i
        self.info[:, 1] = i * cols + j
        self.info[:, 2] = t
        self.q_spans = [span(bounds[w], bounds[w + 1], n, 8) for w in range(3)]
        self.slots = [[], [], []]
        half = 2 * rows * m
        ranges = {0: [(w, bounds[w], bounds[w + 1]) for w in range(3)]}
        ranges[1] = ranges[0]
        ranges[2] = [(0, 0, half), (2, half, 2 * half)]
        self.used = [0, 0, 0]
        for g in range(3):
            for w, low, high in ranges[g]:
                low, high = int(low), int(high)
                first, size = (int(x) for x in span(low, high, n, 16))
                base = self.used[w]
                self.slots[g].append((w, first, size, base))
                self.info[g * n + low : g * n + high, 3 + w] = base + np.arange(low, high) - first
                self.used[w] += size
        assert max(self.used) <= LANES


def attention(plan, latents, queries, kw, vw, allowed_of, units, found):
    width = queries.shape[1]
    head_dim = width // HEADS
    n = plan.own
    group = LANES // head_dim
    lane = lax.broadcasted_iota(jnp.int32, (1, LANES), 1)
    lane_head = [(lane >= h * head_dim) & (lane < (h + 1) * head_dim) for h in range(group)]
    low_half = lane < LANES // 2
    odd = add_all([jnp.where(lane_head[h], 1.0, 0.0) for h in range(1, group, 2)])
    halves = [(1.0 - odd).astype(BF16), odd.astype(BF16)]
    sets = {}
    for p in range(latents):
        sets.setdefault((p + 1) // 2, []).append(p)
    sets = list(sets.values())
    def scores(g, w):
        cut = slice(g * LANES, (g + 1) * LANES)
        first, size = plan.q_spans[w]
        raised = []
        for members in sets:
            parts = [queries[p * n + first : p * n + first + size, cut] for p in members]
            base = jnp.concatenate(parts, axis=0)
            if len(members) == 2:
                stack = jnp.concatenate([jnp.where(h, base, 0.0) for h in lane_head], axis=0)
                keys = jnp.concatenate([kw[w, p, :, cut] for p in members], axis=0)
            else:
                stack = jnp.concatenate(
                    [jnp.where(low_half, base, 0.0), jnp.where(low_half, 0.0, base)], axis=0
                )
                keys = jnp.concatenate([kw[w, members[0], :, cut] * h for h in halves], axis=0)
            raised.append(mm_nt(stack.astype(BF16), keys))
        return raised

    def mixed(g, w, raised):
        cut = slice(g * LANES, (g + 1) * LANES)
        first, size = plan.q_spans[w]
        weights = []
        for members, score in zip(sets, raised):
            allowed = jnp.concatenate([allowed_of(w)] * (score.shape[0] // size), axis=0) > 0.5
            left = jnp.where(allowed, jnp.exp(score[:, :LANES]), 0.0)
            right = jnp.where(allowed, jnp.exp(score[:, LANES:]), 0.0)
            if len(members) == 2:
                inverse = 1.0 / jnp.sum(left + right, axis=1, keepdims=True)
                left, right = left * inverse, right * inverse
            else:
                left = left * (1.0 / jnp.sum(left, axis=1, keepdims=True))
                right = right * (1.0 / jnp.sum(right, axis=1, keepdims=True))
            weights.append(jnp.concatenate([left, right], axis=1).astype(BF16))
        for members, weight in zip(sets, weights):
            many = len(members) * size
            if len(members) == 2:
                values = jnp.concatenate([vw[w, p, :, cut] for p in members], axis=0)
                total = mm(weight, values)
                piece = total[:many]
                for h in range(1, group):
                    piece = jnp.where(lane_head[h], total[h * many : (h + 1) * many], piece)
            else:
                values = jnp.concatenate([vw[w, members[0], :, cut] * h for h in halves], axis=0)
                total = mm(weight, values)
                piece = jnp.where(low_half, total[:many], total[many:])
            for k, p in enumerate(members):
                found[p, g, w] = piece[k * size : (k + 1) * size]

    ahead = [scores(*unit) for unit in units[:AHEAD]]
    yield
    for k, unit in enumerate(units):
        if k + AHEAD < len(units):
            ahead.append(scores(*units[k + AHEAD]))
        mixed(*unit, ahead.pop(0))
        yield


def run(works):
    waiting, live = [iter(work) for work in works], []
    while waiting or live:
        if waiting:
            live.append(waiting.pop(0))
        for work in list(live):
            if next(work, run) is run:
                live.remove(work)


def front_kernel(
    plan, names, sizes,
    patches, weight, level_embed, ids, labels, cross_gain, lq, swin_gain, info_in, code_in, hm_in,
    cross_query, cross_kv, cross_out, swin_qkv, swin_out, mlp_up, mlp_down,
    start, queries, kw, vw, mask, early, o_so, o_up, o_down,
    pbuf, wbuf, lebuf, idbuf, labbuf, cgain, lqbuf, sgain, info, codes, hm,
    b_query, b_kv, b_out, b_qkv, buf, wide, kq, sems, wsems, send, recv,
):
    rows, cols, cap = plan.rows, plan.cols, plan.cap
    levels, lat_count, lon_count = sizes
    bands = levels
    width = weight.shape[1]
    latents = lq.shape[0]
    head_dim = width // HEADS
    inv_root = 1.0 / math.sqrt(head_dim)
    tile_rows = plan.tile_rows
    n = plan.own

    pairs = [
        (ids, idbuf), (labels, labbuf), (patches, pbuf), (weight, wbuf), (level_embed, lebuf),
        (cross_gain, cgain), (lq, lqbuf), (swin_gain, sgain), (info_in, info), (code_in, codes),
        (hm_in, hm), (cross_query, b_query), (cross_kv, b_kv), (cross_out, b_out),
        (swin_qkv, b_qkv), (swin_out, o_so), (mlp_up, o_up), (mlp_down, o_down),
    ]
    loads = [
        None if k == 3 else pltpu.make_async_copy(a, b, sems.at[k]) for k, (a, b) in enumerate(pairs)
    ]
    features = weight.shape[0]
    chunks = [(k, min(KCUT, features - k)) for k in range(0, features, KCUT)]
    pieces = [
        pltpu.make_async_copy(weight.at[pl.ds(k, size)], wbuf.at[pl.ds(k, size)], wsems.at[i])
        for i, (k, size) in enumerate(chunks)
    ]
    for k in (0, 1, 2):
        loads[k].start()
    for piece in pieces:
        piece.start()
    for k in (4, 5):
        loads[k].start()

    me_l, me_a, me_o = (lax.axis_index(name) for name in names)
    partner = me_a + 1 - 2 * lax.rem(me_a, 2)
    lats = (me_a, partner)
    lons = {
        0: me_o,
        1: lax.rem(me_o + 1, lon_count),
        -1: lax.rem(me_o + lon_count - 1, lon_count),
    }
    band_of = [lax.rem(me_l + dm, levels) for dm in range(levels)]
    direct = [(dm, 0) for dm in range(1, levels)] + [(dm, 1) for dm in range(levels)]
    targets = [(band_of[dm], lats[da], me_o) for dm, da in direct]
    sides = [(da, do) for da in (0, 1) for do in (1, -1)]
    beside = {(da, do): (me_l, lats[da], lons[do]) for da, do in sides}
    inner = {1: me_o < lon_count - 1, -1: me_o > 0}
    barrier = pltpu.get_barrier_semaphore()
    for target in targets:
        pl.semaphore_signal(barrier, inc=1, device_id=target, device_id_type=MESH)
    for do in (1, -1):

        @pl.when(inner[do])
        def _():
            for da in (0, 1):
                pl.semaphore_signal(barrier, inc=1, device_id=beside[da, do], device_id_type=MESH)

    def step_of(inner_row):
        return add_all([(inner_row >= k * cap).astype(jnp.int32) for k in range(1, BLOCK // cap + 1)])

    def locate(place):
        inner_row, base, held = place, jnp.zeros_like(place), place < 0
        for first, group in zip(plan.starts, plan.groups):
            inner_row = jnp.where(place >= first, place - first, inner_row)
            base = jnp.where(place >= first, group[0], base)
            held = held | ((place >= first) & (place < first + cap * len(group)))
        step = step_of(inner_row)
        return base + step, inner_row - step * cap, held

    row = lax.broadcasted_iota(jnp.int32, (tile_rows, 1), 0)
    col_of, slot_of, used = locate(row)
    meta_row = (row == BLOCK - 1) | (row == tile_rows - 1)
    lane = lax.broadcasted_iota(jnp.int32, (1, LANES), 1)
    lane_row = lane
    for k in range(1, len(plan.planes[0])):
        lane_row = jnp.where(lane >= k * tile_rows, lane - k * tile_rows, lane_row)
    _, lane_slot, _ = locate(lane_row)
    lane_in = jnp.bitwise_and(lane, BLOCK - 1)
    halo_slot = lane_in - step_of(lane_in) * cap
    cell = lax.broadcasted_iota(jnp.int32, (LANES, 1), 0)
    cell_i = add_all([(cell >= k * cols).astype(jnp.int32) for k in range(1, rows)])
    cell_j = cell - cell_i * cols
    picked_j = lax.broadcasted_iota(jnp.int32, (LANES, cols), 1) == cell_j
    eye = lax.broadcasted_iota(jnp.int32, (LANES, LANES), 0) == lax.broadcasted_iota(
        jnp.int32, (LANES, LANES), 1
    )
    loads[0].wait()
    loads[1].wait()
    lab = labbuf[...].astype(F32)
    col_lab = jnp.zeros((LANES, cols), F32)
    for k in range(rows):
        col_lab = jnp.where(cell_i == k, lab[k : k + 1, :], col_lab)
    lab_col = jnp.sum(jnp.where(picked_j, col_lab, 0.0), axis=1, keepdims=True)
    lab_row = jnp.sum(jnp.where(eye, lab_col, 0.0), axis=0, keepdims=True)
    picks, metas = [], []
    cells_all = rows * cols * bands
    source = lax.broadcasted_iota(jnp.int32, (tile_rows, cells_all), 1)
    for band in range(bands):
        id_col = jnp.full((tile_rows, 1), -1, jnp.int32)
        id_row = jnp.full((1, LANES), -1, jnp.int32)
        halo_row = jnp.full((1, LANES), -1, jnp.int32)
        for s in range(cap):
            number = idbuf[0, band, 0, 0, s]
            id_col = jnp.where(slot_of == s, number, id_col)
            id_row = jnp.where(lane_slot == s, number, id_row)
            halo_row = jnp.where(halo_slot == s, number, halo_row)
        wanted = jnp.where(used & (id_col >= 0), (id_col * cols + col_of) * bands + band, -1)
        picks.append(jnp.where(source == wanted, 1.0, 0.0))
        pad = jnp.zeros((1, width - 3 * LANES), F32)
        metas.append(jnp.concatenate([id_row.astype(F32), lab_row, halo_row.astype(F32), pad], axis=1))
    pick = jnp.concatenate(picks, axis=0).astype(BF16)
    loads[2].wait()
    cells_in = pbuf[...].reshape(cells_all, patches.shape[-1])
    cells_in = mm(pick, cells_in).astype(BF16)
    products = []
    for piece, (k, size) in zip(pieces, chunks):
        piece.wait()
        products.append(mm(cells_in[:, k : k + size], wbuf[k : k + size]))
    for load in loads[6:]:
        load.start()
    loads[4].wait()
    embedded = (add_all(products) + lebuf[...]).astype(BF16).astype(F32)
    loads[5].wait()
    listed = layer_norm(embedded, cgain[...])
    for band in range(bands):
        part = listed[band * tile_rows : (band + 1) * tile_rows]
        buf[band] = jnp.where(meta_row, metas[band], part).astype(BF16)
    pl.semaphore_wait(barrier, len(targets) + 2 * add_all([inner[do].astype(jnp.int32) for do in (1, -1)]))
    copies = {}
    for k, (dm, da) in enumerate(direct):
        copies[dm, da] = pltpu.make_async_remote_copy(
            src_ref=buf.at[band_of[dm]],
            dst_ref=wide.at[me_l, pl.ds(plan.tiles[da][0], tile_rows)],
            send_sem=send.at[k],
            recv_sem=recv.at[k],
            device_id=targets[k],
            device_id_type=MESH,
        )
    relays = {}
    for dm in range(levels):
        level = lax.rem(me_l + dm, levels)
        for da, do in sides:
            origin = tile_rows - BLOCK if do == 1 else 0
            target = plan.tiles[(2 if do == 1 else 4) + da][0]
            slot = len(direct) + len(relays)
            relays[dm, da, do] = pltpu.make_async_remote_copy(
                src_ref=(wide if dm else buf).at[level, pl.ds(origin, BLOCK)],
                dst_ref=wide.at[level, pl.ds(target, BLOCK)],
                send_sem=send.at[slot],
                recv_sem=recv.at[slot],
                device_id=beside[da, do],
                device_id_type=MESH,
            )
    near = [move for move in direct if move[0] == 0 or move[1] == 0]
    far = [move for move in direct if move not in near]
    for move in near:
        copies[move].start()
    for da, do in sides:
        pl.when(inner[do])(relays[0, da, do].start)
    wide[me_l, pl.ds(0, tile_rows)] = buf[me_l]
    for side, (first, count) in ((-1, (2, 2)), (1, (4, 2))):

        @pl.when(jnp.logical_not(inner[side]))
        def _():
            low = plan.tiles[first][0]
            wide[:, low : low + count * BLOCK] = jnp.zeros((levels, count * BLOCK, width), BF16)


    for w in range(3):
        for p in range(latents):
            if plan.used[w] < LANES:
                fill = jnp.zeros((LANES - plan.used[w], width), BF16)
                kw[w, p, plan.used[w] :] = fill
                vw[w, p, plan.used[w] :] = fill
    for move in far:
        copies[move].start()
    for load in loads[6:11]:
        load.wait()
    lq_f = lqbuf[...].astype(F32)
    hm_f = hm[...].astype(F32)
    loads[11].wait()
    cq = (mm(lqbuf[...], b_query[...]) * inv_root).astype(BF16).astype(F32)
    masked = jnp.concatenate([cq[q : q + 1] * hm_f for q in range(latents)], axis=0).astype(BF16)
    loads[12].wait()
    kq[...] = mm_nt(b_kv[:, :width], masked).astype(BF16)
    loads[13].wait()
    loads[14].wait()

    def head(g):
        part = plan.parts[g]
        code_c = info[g * n : (g + 1) * n, 0:1]
        low = plan.tiles[part[0]][0]
        size = sum(plan.tiles[t][1] for t in part)
        exps, values = [], []
        for plane in plan.planes:
            tokens = [wide[l, low : low + size].astype(F32) for l in plane]
            tokens = jnp.concatenate(tokens, axis=0).astype(BF16)
            id_row = jnp.full((1, LANES), -1.0, F32)
            begin = 0
            for l in plane:
                for t in part:
                    meta = plan.tiles[t][0]
                    ids_at = 2 * LANES if g == 2 else 0
                    line = wide[l, meta : meta + BLOCK, ids_at : ids_at + LANES]
                    line = line.astype(F32)[BLOCK - 1 :]
                    id_row = jnp.where(lane >= begin, line, id_row)
                    begin += plan.tiles[t][1]
            id_row = id_row.astype(jnp.int32)
            code_r = jnp.where(id_row >= 0, codes[g : g + 1, :] + id_row, -1)
            pick = jnp.where(code_c == code_r, 1.0, 0.0)[:, :begin]
            keys_in = mm(pick.astype(BF16), tokens).astype(BF16)
            yield
            present = jnp.sum(pick, axis=1, keepdims=True)
            score = mm(keys_in, kq[...])
            values.append(mm(keys_in, b_kv[:, width:]))
            yield
            exps.append(jnp.exp(score) * present)
        norm = add_all(exps)
        norm = jnp.where(norm > 0.0, norm, 1.0)
        wide_weights = []
        for e in exps:
            share = (e / norm).astype(BF16).astype(F32)
            wide_weights.append(jnp.concatenate([share, jnp.zeros_like(share)], axis=1))
        mixers[g] = wide_weights, values

    def tail(g, picked):
        weights, values = mixers[g]
        low, high = picked[0] * width, (picked[-1] + 1) * width
        mixes = []
        for weight, v in zip(weights, values):
            cuts = []
            for p in picked:
                spread = []
                for c in range(width // LANES):
                    where = jnp.broadcast_to(p * HEADS + (c * LANES + lane) // head_dim, (n, LANES))
                    spread.append(jnp.take_along_axis(weight, where, axis=1))
                cuts.append(jnp.concatenate(spread, axis=1) * v)
            mixes.append(jnp.concatenate(cuts, axis=0))
        out = mm(add_all(mixes).astype(BF16), b_out[...])
        yield
        latent = jnp.concatenate(
            [out[k * n : (k + 1) * n] + lq_f[p : p + 1] for k, p in enumerate(picked)], axis=0
        )
        normed = layer_norm(latent, sgain[...]).astype(BF16)
        if g == 0:
            start[picked[0] * n : (picked[-1] + 1) * n] = latent
            asked = mm(normed, b_qkv[:, :width])
        keys = mm(normed, b_qkv[:, width : 2 * width])
        values = mm(normed, b_qkv[:, 2 * width :])
        yield
        if g == 0:
            queries[picked[0] * n : (picked[-1] + 1) * n] = asked * inv_root
        for k, p in enumerate(picked):
            for w, first, size, base in plan.slots[g]:
                cut = slice(k * n + first, k * n + first + size)
                kw[w, p, base : base + size] = keys[cut].astype(BF16)
                vw[w, p, base : base + size] = values[cut].astype(BF16)

    lab_cols, lab_keys = {}, {}

    def labels_of(g):
        cells = slice(g * n, (g + 1) * n)
        tile_c = info[cells, 2:3]
        seg = jnp.zeros((n, LANES), F32)
        for t in plan.parts[g]:
            first = plan.tiles[t][0]
            line = wide[me_l, first : first + BLOCK, LANES : 2 * LANES].astype(F32)[BLOCK - 1 :]
            seg = jnp.where(tile_c == t, line, seg)
        lab_cols[g] = jnp.sum(jnp.where(lane == info[cells, 1:2], seg, 0.0), axis=1, keepdims=True)
        lab_keys[g] = lab_cols[g]
        if g == 2:
            outside = (tile_c < 4) & (me_o == 0) | (tile_c >= 4) & (me_o == lon_count - 1)
            lab_keys[g] = jnp.where(outside, -1.0, lab_cols[g])
        yield

    at_of = [sum(size for _, size in plan.q_spans[:w]) for w in range(3)]

    def view(groups, windows):
        for g in groups:
            yield from labels_of(g)
        for w in windows:
            first, size = plan.q_spans[w]
            keys = [
                jnp.where(lane == info[g * n : (g + 1) * n, 3 + w : 4 + w], lab_keys[g] + 1.0, 0.0)
                for g in sorted(lab_keys)
            ]
            keys = jnp.sum(add_all(keys), axis=0, keepdims=True) - 1.0
            seen = jnp.where(lab_cols[0][first : first + size] == keys, 1.0, 0.0)
            mask[at_of[w] : at_of[w] + size] = seen
            yield

    def allowed_of(w):
        return mask[at_of[w] : at_of[w] + plan.q_spans[w][1]]

    def halo():
        yield from head(2)
        yield from tail(2, halves[0])

    found = {}
    units = [(g, 1) for g in range(width // LANES)]
    mixers = {}
    half = -(-latents // 2)
    halves = [list(range(latents))]
    for move in direct:
        if move[1] == 0:
            copies[move].wait_recv()
    for (dm, _, do), relay in relays.items():
        if dm:
            pl.when(inner[do])(relay.start)
    run([head(0)])
    run([tail(0, picked) for picked in halves])
    for move in direct:
        if move[1] == 1:
            copies[move].wait_recv()
    run([head(1), view([0, 1], [1])])
    run([tail(1, picked) for picked in halves])
    for (dm, _, do), relay in relays.items():
        pl.when(inner[-do])(relay.wait_recv)
    run([halo(), attention(plan, latents, queries, kw, vw, allowed_of, units, found), view([2], [0, 2])])
    for (p, g, _), piece in found.items():
        early[p, :, g * LANES : (g + 1) * LANES] = piece

    for copy in copies.values():
        copy.wait_send()
    for (_, _, do), relay in relays.items():
        pl.when(inner[do])(relay.wait_send)
    for load in loads[15:]:
        load.wait()


def back_kernel(plan, start, queries, kw, vw, mask, early, gain, b_so, b_up, b_down, out, obuf, sems):
    width = b_so.shape[0]
    n = plan.own
    latents = start.shape[0] // n
    masks, at = [], 0
    for first, size in plan.q_spans:
        masks.append(mask[at : at + size])
        at += size
    found = {}
    row = lax.broadcasted_iota(jnp.int32, (8, 1), 0)

    def merged(p, g):
        tiles = []
        for r in range(0, n, 8):
            tile = None
            for w, (first, size) in enumerate(plan.q_spans):
                if plan.bounds[w] < r + 8 and plan.bounds[w + 1] > r:
                    here = found[p, g, w][r - first : r - first + 8]
                    tile = here if tile is None else jnp.where(row + r < plan.bounds[w], tile, here)
            tiles.append(tile)
        return jnp.concatenate(tiles, axis=0)

    whole = {}
    parts = [(0, n)]
    runs, k = [], 0
    while k < n:
        i, j, w = plan.own_cells[k]
        size = 1
        while (
            k + size < n
            and plan.own_cells[k + size] == (i, j + size, w)
            and not any(k + size == low for low, _ in parts)
        ):
            size += 1
        runs.append((k, size, i * plan.cols + j))
        k += size
    writes = [
        pltpu.make_async_copy(
            obuf.at[pl.ds(first, size)], out.at[pl.ds(target, size)], sems.at[k]
        )
        for k, (first, size, target) in enumerate(runs)
    ]
    step = 512

    def tail(low, high):
        size = high - low
        mix = jnp.concatenate([whole[p][low:high] for p in range(latents)], axis=0).astype(BF16)
        base = [start[p * n + low : p * n + high] for p in range(latents)]
        result = jnp.concatenate(base, axis=0) + mm(mix, b_so[...])
        yield
        mlp_in = layer_norm(result, gain[...]).astype(BF16)
        chunks = list(range(0, b_up.shape[1], step))
        ahead = mm(mlp_in, b_up[:, :step])
        yield
        for c in chunks:
            up = ahead
            if c + step < b_up.shape[1]:
                ahead = mm(mlp_in, b_up[:, c + step : c + 2 * step])
            act = (up * (1.0 + lax.erf(up * math.sqrt(0.5))) * 0.5).astype(BF16)
            result = result + mm(act, b_down[c : c + step, :])
            yield
        for p in range(latents):
            obuf[low:high, p, :] = result[p * size : (p + 1) * size]
        for write, (first, _, _) in zip(writes, runs):
            if low <= first < high:
                write.start()

    groups = range(width // LANES)
    for p in range(latents):
        for g in groups:
            found[p, g, 1] = early[p, :, g * LANES : (g + 1) * LANES]
    units = [(g, w) for g in groups for w in (0, 2)]
    run([attention(plan, latents, queries, kw, vw, masks.__getitem__, units, found)])
    for p in range(latents):
        whole[p] = jnp.concatenate([merged(p, g) for g in groups], axis=1)
    run([tail(low, high) for low, high in parts])
    for write in writes:
        write.wait()


def shards(
    sizes, names,
    patches, level_embed, embed_weight, block_ids, latent_queries, cross_gain, cross_query, cross_kv,
    cross_out, region_ids, swin_gain, swin_qkv, swin_out, mlp_gain, mlp_up, mlp_down,
):
    levels = sizes[0]
    _, bands, rows, cols, features = patches.shape
    assert bands == levels
    width = embed_weight.shape[1]
    latents = latent_queries.shape[0]
    plan = Plan(rows, cols, block_ids.shape[-1], levels)
    n = plan.own
    head_mask = np.arange(width)[None, :] // (width // HEADS) == np.arange(HEADS)[:, None]
    vmem = pl.BlockSpec(memory_space=pltpu.VMEM)
    hbm = pl.BlockSpec(memory_space=pl.ANY)
    moves = 6 * levels - 1
    q_rows = sum(size for _, size in plan.q_spans)
    handed = [
        ((latents * n, width), F32), ((latents * n, width), F32),
        ((3, latents, LANES, width), BF16), ((3, latents, LANES, width), BF16),
        ((q_rows, LANES), F32), ((latents, plan.q_spans[1][1], width), F32),
        (swin_out.shape, BF16), (mlp_up.shape, BF16), (mlp_down.shape, BF16),
    ]
    room = int(sum(math.prod(shape) * np.dtype(kind).itemsize for shape, kind in handed))
    inputs = (
        patches[0].transpose(1, 2, 0, 3), embed_weight, level_embed, block_ids, region_ids,
        cross_gain.reshape(1, -1), latent_queries, swin_gain.reshape(1, -1),
        jnp.asarray(plan.info), jnp.asarray(plan.row_code), jnp.asarray(head_mask, BF16),
    )
    weights = (cross_query, cross_kv, cross_out, swin_qkv)
    later = (swin_out, mlp_up, mlp_down)
    held = [pltpu.VMEM(x.shape, x.dtype) for x in inputs]
    held[3] = pltpu.SMEM(block_ids.shape, jnp.int32)
    outs = pl.pallas_call(
        functools.partial(front_kernel, plan, names, sizes),
        out_shape=[pltpu.VMEM(shape, kind) for shape, kind in handed],
        in_specs=[hbm] * 18,
        out_specs=[vmem] * len(handed),
        scratch_shapes=held
        + [pltpu.VMEM(w.shape, BF16) for w in weights]
        + [
            pltpu.VMEM((bands, plan.tile_rows, width), BF16),
            pltpu.VMEM((levels, plan.wide_rows, width), BF16),
            pltpu.VMEM((width, latents * HEADS), BF16),
            pltpu.SemaphoreType.DMA((18,)),
            pltpu.SemaphoreType.DMA((-(-features // KCUT),)),
            pltpu.SemaphoreType.DMA((moves,)),
            pltpu.SemaphoreType.DMA((moves,)),
        ],
        compiler_params=pltpu.CompilerParams(
            collective_id=0, has_side_effects=True, vmem_limit_bytes=VMEM - room
        ),
        name="front",
    )(*inputs, *weights, *later)
    outs = [pltpu.with_memory_space_constraint(x, pltpu.VMEM) for x in outs]
    tokens = pl.pallas_call(
        functools.partial(back_kernel, plan),
        out_shape=jax.ShapeDtypeStruct((n, latents, width), F32),
        in_specs=[vmem] * 10,
        out_specs=hbm,
        scratch_shapes=[
            pltpu.VMEM((n, latents, width), F32),
            pltpu.SemaphoreType.DMA((4 * rows,)),
        ],
        compiler_params=pltpu.CompilerParams(vmem_limit_bytes=40 << 20),
        name="back",
    )(*outs[:6], mlp_gain.reshape(1, -1), *outs[6:])
    return tokens.reshape(rows, cols, latents, width).transpose(2, 0, 1, 3)


def solution(mesh):
    names = ("lvl", "lat", "lon")
    sizes = tuple(mesh.shape[name] for name in names)
    tiled = P("lvl", None, "lat", "lon", None)
    return jax.shard_map(
        functools.partial(shards, sizes, names),
        mesh=mesh,
        in_specs=(
            tiled, P("lvl", None), P(), tiled, P(), P(), P(), P(), P(), P(("lvl", "lat"), "lon"),
            P(), P(), P(), P(), P(), P(),
        ),
        out_specs=P(None, ("lvl", "lat"), "lon", None),
        check_vma=False,
    )
```

time: 18 us -> 17.2 us (0.956)
  the two profiles are of different devices: /device:TPU:0 before, /device:TPU:1 now
where the time goes in v4:
time: 17.2 us; the launch traced here: 17.1 us
  Pallas kernels  17 us (99%)
    pallas_call x1, Pallas kernels, shards(): pl.pallas_call(functools.partial(front_kernel, plan, names, sizes), out_s...  13 us
    pallas_call x1, Pallas kernels, shards(): pl.pallas_call(functools.partial(back_kernel, plan), out_shape=jax.ShapeD...  4.06 us

profile of v4, /device:TPU:1, one launch (start us, length us, event | category | flops | bytes accessed | tf_op | source)
XLA Modules:
  0.0 17.1 jit_solution(15180803725723253892)
XLA Ops:
  0.0 0.0 copy-start
  0.0 13.0 %front.1 = (f32[288,512]{1,0:T(8,128)S(1)}, f32[288,512]{1,0:T(8,128)S(1)}, bf16[3,4,128,512]{3,2,1,0:T(8,128)(2,1)S(1)}, bf16[3,4,128,512]{3,2,1,0:T(8,128)(2,1...) custom-call(bf16[6,12,2,1000]{3,2,1,0:T(2,128)(2,1)} %bitcast.10, ...), custom_call_target="tpu_custom_call" | custom-call | tf_op jit(solution)/shard_map/front/pallas_call | solution.py:656
  13.0 0.0 copy-done
  13.0 4.1 %back.1 = f32[72,4,512]{2,1,0:T(4,128)} custom-call(f32[288,512]{1,0:T(8,128)S(1)} %get-tuple-element.14.start, f32[288,512]{1,0:T(8,128)S(1)} %get-tuple-element.15.queries, bf16[3,4,128,512]{3,2,1,0:T(8,128)(2,1)S(1)} %get-tuple-element.16.kw, bf16[3,4,128,512]{3,2,1,0:T(8,128)(2,1)S(1)} %get-tuple-element.17.vw, f32[88,128]{1,0:T(8,128)S(1)} %get-tuple-element.18.mask, ...), custom_call_target="tpu_custom_call" | custom-call | tf_op jit(solution)/shard_map/back/pallas_call | solution.py:678
Async XLA Ops:
  0.0 13.0 %copy-start = (f32[512]{0:T(512)S(1)}, f32[512]{0:T(512)}, u32[]{:S(2)}) copy-start(f32[512]{0:T(512)} %param.32) | copy-start | bytes 6148

commit v5 on v4

--- a/solution.py
+++ b/solution.py
@@ -122,7 +122,7 @@
         assert max(self.used) <= LANES
 
 
-def attention(plan, latents, queries, kw, vw, allowed_of, units, found):
+def attention(plan, latents, queries, kw, vw, allowed_of, units, found, early=AHEAD):
     width = queries.shape[1]
     head_dim = width // HEADS
     n = plan.own
@@ -184,11 +184,11 @@
             for k, p in enumerate(members):
                 found[p, g, w] = piece[k * size : (k + 1) * size]
 
-    ahead = [scores(*unit) for unit in units[:AHEAD]]
+    ahead = [scores(*unit) for unit in units[:early]]
     yield
     for k, unit in enumerate(units):
-        if k + AHEAD < len(units):
-            ahead.append(scores(*units[k + AHEAD]))
+        if k + early < len(units):
+            ahead.append(scores(*units[k + early]))
         mixed(*unit, ahead.pop(0))
         yield
 
@@ -328,7 +328,7 @@
     for piece, (k, size) in zip(pieces, chunks):
         piece.wait()
         products.append(mm(cells_in[:, k : k + size], wbuf[k : k + size]))
-    for load in loads[6:]:
+    for load in loads[6:15]:
         load.start()
     loads[4].wait()
     embedded = (add_all(products) + lebuf[...]).astype(BF16).astype(F32)
@@ -355,20 +355,23 @@
             origin = tile_rows - BLOCK if do == 1 else 0
             target = plan.tiles[(2 if do == 1 else 4) + da][0]
             slot = len(direct) + len(relays)
+            held_by_me = dm == 0 and da == 1
             relays[dm, da, do] = pltpu.make_async_remote_copy(
-                src_ref=(wide if dm else buf).at[level, pl.ds(origin, BLOCK)],
+                src_ref=wide.at[level, pl.ds(plan.tiles[1][0] + origin, BLOCK)]
+                if held_by_me
+                else (wide if dm else buf).at[level, pl.ds(origin, BLOCK)],
                 dst_ref=wide.at[level, pl.ds(target, BLOCK)],
                 send_sem=send.at[slot],
                 recv_sem=recv.at[slot],
-                device_id=beside[da, do],
+                device_id=beside[0 if held_by_me else da, do],
                 device_id_type=MESH,
             )
     near = [move for move in direct if move[0] == 0 or move[1] == 0]
     far = [move for move in direct if move not in near]
     for move in near:
         copies[move].start()
-    for da, do in sides:
-        pl.when(inner[do])(relays[0, da, do].start)
+    for do in (1, -1):
+        pl.when(inner[do])(relays[0, 0, do].start)
     wide[me_l, pl.ds(0, tile_rows)] = buf[me_l]
     for side, (first, count) in ((-1, (2, 2)), (1, (4, 2))):
 
@@ -519,16 +522,22 @@
     for (dm, _, do), relay in relays.items():
         if dm:
             pl.when(inner[do])(relay.start)
+    copies[0, 1].wait_recv()
+    for do in (1, -1):
+        pl.when(inner[do])(relays[0, 1, do].start)
+    for load in loads[15:]:
+        load.start()
     run([head(0)])
     run([tail(0, picked) for picked in halves])
     for move in direct:
-        if move[1] == 1:
+        if move[0] and move[1]:
             copies[move].wait_recv()
     run([head(1), view([0, 1], [1])])
     run([tail(1, picked) for picked in halves])
+    run([attention(plan, latents, queries, kw, vw, allowed_of, units, found)])
     for (dm, _, do), relay in relays.items():
         pl.when(inner[-do])(relay.wait_recv)
-    run([halo(), attention(plan, latents, queries, kw, vw, allowed_of, units, found), view([2], [0, 2])])
+    run([halo(), view([2], [0, 2])])
     for (p, g, _), piece in found.items():
         early[p, :, g * LANES : (g + 1) * LANES] = piece
 
@@ -563,7 +572,8 @@
         return jnp.concatenate(tiles, axis=0)
 
     whole = {}
-    parts = [(0, n)]
+    middle = n // 16 * 8 + 8
+    parts = [(0, middle), (middle, n)] if middle < n else [(0, n)]
     runs, k = [], 0
     while k < n:
         i, j, w = plan.own_cells[k]
@@ -584,38 +594,38 @@
     ]
     step = 512
 
-    def tail(low, high):
-        size = high - low
-        mix = jnp.concatenate([whole[p][low:high] for p in range(latents)], axis=0).astype(BF16)
-        base = [start[p * n + low : p * n + high] for p in range(latents)]
-        result = jnp.concatenate(base, axis=0) + mm(mix, b_so[...])
-        yield
+    def finish():
+        mix = jnp.concatenate([whole[p] for p in range(latents)], axis=0).astype(BF16)
+        result = start[...] + mm(mix, b_so[...])
         mlp_in = layer_norm(result, gain[...]).astype(BF16)
         chunks = list(range(0, b_up.shape[1], step))
         ahead = mm(mlp_in, b_up[:, :step])
-        yield
         for c in chunks:
             up = ahead
             if c + step < b_up.shape[1]:
                 ahead = mm(mlp_in, b_up[:, c + step : c + 2 * step])
-            act = (up * (1.0 + lax.erf(up * math.sqrt(0.5))) * 0.5).astype(BF16)
-            result = result + mm(act, b_down[c : c + step, :])
-            yield
-        for p in range(latents):
-            obuf[low:high, p, :] = result[p * size : (p + 1) * size]
-        for write, (first, _, _) in zip(writes, runs):
-            if low <= first < high:
-                write.start()
+            act = up * (1.0 + lax.erf(up * math.sqrt(0.5))) * 0.5
+            if c != chunks[-1]:
+                result = result + mm(act.astype(BF16), b_down[c : c + step, :])
+        for low, high in parts:
+            cuts = [slice(p * n + low, p * n + high) for p in range(latents)]
+            done = jnp.concatenate([act[cut] for cut in cuts], axis=0).astype(BF16)
+            done = jnp.concatenate([result[cut] for cut in cuts], axis=0) + mm(done, b_down[c:, :])
+            for p in range(latents):
+                obuf[low:high, p, :] = done[p * (high - low) : (p + 1) * (high - low)]
+            for write, (first, _, _) in zip(writes, runs):
+                if low <= first < high:
+                    write.start()
 
     groups = range(width // LANES)
     for p in range(latents):
         for g in groups:
             found[p, g, 1] = early[p, :, g * LANES : (g + 1) * LANES]
     units = [(g, w) for g in groups for w in (0, 2)]
-    run([attention(plan, latents, queries, kw, vw, masks.__getitem__, units, found)])
+    run([attention(plan, latents, queries, kw, vw, masks.__getitem__, units, found, 3)])
     for p in range(latents):
         whole[p] = jnp.concatenate([merged(p, g) for g in groups], axis=1)
-    run([tail(low, high) for low, high in parts])
+    finish()
     for write in writes:
         write.wait()
 

time: 17.2 us -> 16.9 us (0.983)
  Pallas kernels: 17 us -> 16.7 us
    pallas_call x1, Pallas kernels: 13 us -> 12.8 us  [shards(): pl.pallas_call(functools.partial(front_kernel, plan, names, sizes), out_s...]
where the time goes in v5:
time: 16.9 us; the launch traced here: 16.7 us
  Pallas kernels  16.7 us (99%)
    pallas_call x1, Pallas kernels, shards(): pl.pallas_call(functools.partial(front_kernel, plan, names, sizes), out_s...  12.8 us
    pallas_call x1, Pallas kernels, shards(): pl.pallas_call(functools.partial(back_kernel, plan), out_shape=jax.ShapeD...  3.92 us

profile of v5, /device:TPU:1, one launch (start us, length us, event | category | flops | bytes accessed | tf_op | source)
XLA Modules:
  0.0 16.7 jit_solution(3261990906685074656)
XLA Ops:
  0.0 0.0 copy-start
  0.0 12.8 %front.1 = (f32[288,512]{1,0:T(8,128)S(1)}, f32[288,512]{1,0:T(8,128)S(1)}, bf16[3,4,128,512]{3,2,1,0:T(8,128)(2,1)S(1)}, bf16[3,4,128,512]{3,2,1,0:T(8,128)(2,1...) custom-call(bf16[6,12,2,1000]{3,2,1,0:T(2,128)(2,1)} %bitcast.10, ...), custom_call_target="tpu_custom_call" | custom-call | tf_op jit(solution)/shard_map/front/pallas_call | solution.py:666
  12.8 0.0 copy-done
  12.8 3.9 %back.1 = f32[72,4,512]{2,1,0:T(4,128)} custom-call(f32[288,512]{1,0:T(8,128)S(1)} %get-tuple-element.14.start, f32[288,512]{1,0:T(8,128)S(1)} %get-tuple-element.15.queries, bf16[3,4,128,512]{3,2,1,0:T(8,128)(2,1)S(1)} %get-tuple-element.16.kw, bf16[3,4,128,512]{3,2,1,0:T(8,128)(2,1)S(1)} %get-tuple-element.17.vw, f32[88,128]{1,0:T(8,128)S(1)} %get-tuple-element.18.mask, ...), custom_call_target="tpu_custom_call" | custom-call | tf_op jit(solution)/shard_map/back/pallas_call | solution.py:688
Async XLA Ops:
  0.0 12.8 %copy-start = (f32[512]{0:T(512)S(1)}, f32[512]{0:T(512)}, u32[]{:S(2)}) copy-start(f32[512]{0:T(512)} %param.32) | copy-start | bytes 6148

commit v6 on v5

--- a/solution.py
+++ b/solution.py
@@ -209,7 +209,7 @@
     cross_query, cross_kv, cross_out, swin_qkv, swin_out, mlp_up, mlp_down,
     start, queries, kw, vw, mask, early, o_so, o_up, o_down,
     pbuf, wbuf, lebuf, idbuf, labbuf, cgain, lqbuf, sgain, info, codes, hm,
-    b_query, b_kv, b_out, b_qkv, buf, wide, kq, sems, wsems, send, recv,
+    b_query, b_kv, b_out, b_qkv, buf, wide, kq, own_normed, sems, wsems, send, recv,
 ):
     rows, cols, cap = plan.rows, plan.cols, plan.cap
     levels, lat_count, lon_count = sizes
@@ -264,8 +264,7 @@
 
         @pl.when(inner[do])
         def _():
-            for da in (0, 1):
-                pl.semaphore_signal(barrier, inc=1, device_id=beside[da, do], device_id_type=MESH)
+            pl.semaphore_signal(barrier, inc=1, device_id=beside[0, do], device_id_type=MESH)
 
     def step_of(inner_row):
         return add_all([(inner_row >= k * cap).astype(jnp.int32) for k in range(1, BLOCK // cap + 1)])
@@ -337,7 +336,7 @@
     for band in range(bands):
         part = listed[band * tile_rows : (band + 1) * tile_rows]
         buf[band] = jnp.where(meta_row, metas[band], part).astype(BF16)
-    pl.semaphore_wait(barrier, len(targets) + 2 * add_all([inner[do].astype(jnp.int32) for do in (1, -1)]))
+    pl.semaphore_wait(barrier, len(targets) + add_all([inner[do].astype(jnp.int32) for do in (1, -1)]))
     copies = {}
     for k, (dm, da) in enumerate(direct):
         copies[dm, da] = pltpu.make_async_remote_copy(
@@ -355,7 +354,7 @@
             origin = tile_rows - BLOCK if do == 1 else 0
             target = plan.tiles[(2 if do == 1 else 4) + da][0]
             slot = len(direct) + len(relays)
-            held_by_me = dm == 0 and da == 1
+            held_by_me = da == 1
             relays[dm, da, do] = pltpu.make_async_remote_copy(
                 src_ref=wide.at[level, pl.ds(plan.tiles[1][0] + origin, BLOCK)]
                 if held_by_me
@@ -363,11 +362,13 @@
                 dst_ref=wide.at[level, pl.ds(target, BLOCK)],
                 send_sem=send.at[slot],
                 recv_sem=recv.at[slot],
-                device_id=beside[0 if held_by_me else da, do],
+                device_id=beside[0, do],
                 device_id_type=MESH,
             )
     near = [move for move in direct if move[0] == 0 or move[1] == 0]
     far = [move for move in direct if move not in near]
+    for move in far:
+        copies[move].start()
     for move in near:
         copies[move].start()
     for do in (1, -1):
@@ -387,8 +388,6 @@
                 fill = jnp.zeros((LANES - plan.used[w], width), BF16)
                 kw[w, p, plan.used[w] :] = fill
                 vw[w, p, plan.used[w] :] = fill
-    for move in far:
-        copies[move].start()
     for load in loads[6:11]:
         load.wait()
     lq_f = lqbuf[...].astype(F32)
@@ -459,12 +458,14 @@
         normed = layer_norm(latent, sgain[...]).astype(BF16)
         if g == 0:
             start[picked[0] * n : (picked[-1] + 1) * n] = latent
-            asked = mm(normed, b_qkv[:, :width])
+            own_normed[...] = normed
+            return
         keys = mm(normed, b_qkv[:, width : 2 * width])
         values = mm(normed, b_qkv[:, 2 * width :])
         yield
-        if g == 0:
-            queries[picked[0] * n : (picked[-1] + 1) * n] = asked * inv_root
+        put(g, picked, keys, values)
+
+    def put(g, picked, keys, values):
         for k, p in enumerate(picked):
             for w, first, size, base in plan.slots[g]:
                 cut = slice(k * n + first, k * n + first + size)
@@ -507,6 +508,16 @@
     def allowed_of(w):
         return mask[at_of[w] : at_of[w] + plan.q_spans[w][1]]
 
+    def ask():
+        normed = own_normed[...]
+        asked = mm(normed, b_qkv[:, :width])
+        yield
+        queries[...] = asked * inv_root
+        keys = mm(normed, b_qkv[:, width : 2 * width])
+        values = mm(normed, b_qkv[:, 2 * width :])
+        yield
+        put(0, halves[0], keys, values)
+
     def halo():
         yield from head(2)
         yield from tail(2, halves[0])
@@ -519,21 +530,24 @@
     for move in direct:
         if move[1] == 0:
             copies[move].wait_recv()
-    for (dm, _, do), relay in relays.items():
-        if dm:
+    for (dm, da, do), relay in relays.items():
+        if dm and not da:
             pl.when(inner[do])(relay.start)
-    copies[0, 1].wait_recv()
-    for do in (1, -1):
-        pl.when(inner[do])(relays[0, 1, do].start)
     for load in loads[15:]:
         load.start()
     run([head(0)])
     run([tail(0, picked) for picked in halves])
     for move in direct:
-        if move[0] and move[1]:
+        if move[1]:
             copies[move].wait_recv()
-    run([head(1), view([0, 1], [1])])
-    run([tail(1, picked) for picked in halves])
+    for (_, da, do), relay in relays.items():
+        if da:
+            pl.when(inner[do])(relay.start)
+    def mate():
+        yield from head(1)
+        yield from tail(1, halves[0])
+
+    run([mate(), ask(), view([0, 1], [1])])
     run([attention(plan, latents, queries, kw, vw, allowed_of, units, found)])
     for (dm, _, do), relay in relays.items():
         pl.when(inner[-do])(relay.wait_recv)
@@ -674,6 +688,7 @@
             pltpu.VMEM((bands, plan.tile_rows, width), BF16),
             pltpu.VMEM((levels, plan.wide_rows, width), BF16),
             pltpu.VMEM((width, latents * HEADS), BF16),
+            pltpu.VMEM((latents * n, width), BF16),
             pltpu.SemaphoreType.DMA((18,)),
             pltpu.SemaphoreType.DMA((-(-features // KCUT),)),
             pltpu.SemaphoreType.DMA((moves,)),

time: 16.9 us -> 16.7 us (0.988)
  no operation moved by 1% of the time
where the time goes in v6:
time: 16.7 us; the launch traced here: 16.6 us
  Pallas kernels  16.6 us (99%)
    pallas_call x1, Pallas kernels, shards(): pl.pallas_call(functools.partial(front_kernel, plan, names, sizes), out_s...  12.7 us
    pallas_call x1, Pallas kernels, shards(): pl.pallas_call(functools.partial(back_kernel, plan), out_shape=jax.ShapeD...  3.92 us

profile of v6, /device:TPU:1, one launch (start us, length us, event | category | flops | bytes accessed | tf_op | source)
XLA Modules:
  0.0 16.6 jit_solution(5595751561244715156)
XLA Ops:
  0.0 0.0 copy-start
  0.0 12.7 %front.1 = (f32[288,512]{1,0:T(8,128)S(1)}, f32[288,512]{1,0:T(8,128)S(1)}, bf16[3,4,128,512]{3,2,1,0:T(8,128)(2,1)S(1)}, bf16[3,4,128,512]{3,2,1,0:T(8,128)(2,1...) custom-call(bf16[6,12,2,1000]{3,2,1,0:T(2,128)(2,1)} %bitcast.10, ...), custom_call_target="tpu_custom_call" | custom-call | tf_op jit(solution)/shard_map/front/pallas_call | solution.py:680
  12.7 0.0 copy-done
  12.7 3.9 %back.1 = f32[72,4,512]{2,1,0:T(4,128)} custom-call(f32[288,512]{1,0:T(8,128)S(1)} %get-tuple-element.14.start, f32[288,512]{1,0:T(8,128)S(1)} %get-tuple-element.15.queries, bf16[3,4,128,512]{3,2,1,0:T(8,128)(2,1)S(1)} %get-tuple-element.16.kw, bf16[3,4,128,512]{3,2,1,0:T(8,128)(2,1)S(1)} %get-tuple-element.17.vw, f32[88,128]{1,0:T(8,128)S(1)} %get-tuple-element.18.mask, ...), custom_call_target="tpu_custom_call" | custom-call | tf_op jit(solution)/shard_map/back/pallas_call | solution.py:703
Async XLA Ops:
  0.0 12.7 %copy-start = (f32[512]{0:T(512)S(1)}, f32[512]{0:T(512)}, u32[]{:S(2)}) copy-start(f32[512]{0:T(512)} %param.32) | copy-start | bytes 6148

commit v7 on v6

--- a/solution.py
+++ b/solution.py
@@ -533,16 +533,16 @@
     for (dm, da, do), relay in relays.items():
         if dm and not da:
             pl.when(inner[do])(relay.start)
-    for load in loads[15:]:
-        load.start()
-    run([head(0)])
-    run([tail(0, picked) for picked in halves])
     for move in direct:
         if move[1]:
             copies[move].wait_recv()
     for (_, da, do), relay in relays.items():
         if da:
             pl.when(inner[do])(relay.start)
+    for load in loads[15:]:
+        load.start()
+    run([head(0)])
+    run([tail(0, picked) for picked in halves])
     def mate():
         yield from head(1)
         yield from tail(1, halves[0])

time: 16.7 us -> 16.5 us (0.988)
  the two profiles are of different devices: /device:TPU:1 before, /device:TPU:0 now
where the time goes in v7:
time: 16.5 us; the launch traced here: 16.4 us
  Pallas kernels  16.3 us (99%)
    pallas_call x1, Pallas kernels, shards(): pl.pallas_call(functools.partial(front_kernel, plan, names, sizes), out_s...  12.4 us
    pallas_call x1, Pallas kernels, shards(): pl.pallas_call(functools.partial(back_kernel, plan), out_shape=jax.ShapeD...  3.92 us

profile of v7, /device:TPU:0, one launch (start us, length us, event | category | flops | bytes accessed | tf_op | source)
XLA Modules:
  0.0 16.4 jit_solution(12681231006992537889)
XLA Ops:
  0.0 0.0 copy-start
  0.0 12.4 %front.1 = (f32[288,512]{1,0:T(8,128)S(1)}, f32[288,512]{1,0:T(8,128)S(1)}, bf16[3,4,128,512]{3,2,1,0:T(8,128)(2,1)S(1)}, bf16[3,4,128,512]{3,2,1,0:T(8,128)(2,1...) custom-call(bf16[6,12,2,1000]{3,2,1,0:T(2,128)(2,1)} %bitcast.10, ...), custom_call_target="tpu_custom_call" | custom-call | tf_op jit(solution)/shard_map/front/pallas_call | solution.py:680
  12.4 0.0 copy-done
  12.4 3.9 %back.1 = f32[72,4,512]{2,1,0:T(4,128)} custom-call(f32[288,512]{1,0:T(8,128)S(1)} %get-tuple-element.14.start, f32[288,512]{1,0:T(8,128)S(1)} %get-tuple-element.15.queries, bf16[3,4,128,512]{3,2,1,0:T(8,128)(2,1)S(1)} %get-tuple-element.16.kw, bf16[3,4,128,512]{3,2,1,0:T(8,128)(2,1)S(1)} %get-tuple-element.17.vw, f32[88,128]{1,0:T(8,128)S(1)} %get-tuple-element.18.mask, ...), custom_call_target="tpu_custom_call" | custom-call | tf_op jit(solution)/shard_map/back/pallas_call | solution.py:703
Async XLA Ops:
  0.0 12.4 %copy-start = (f32[512]{0:T(512)S(1)}, f32[512]{0:T(512)}, u32[]{:S(2)}) copy-start(f32[512]{0:T(512)} %param.32) | copy-start | bytes 6148
